TPU v7x, 32 devices: a whole 2x2x4 slice. The times are simulated.
32 devices in a mesh: au: 4 (over z), vert: 4 (over x, core), ch: 2 (over y).
Axes of the slice: x: 2, y: 2, z: 4, core: 2. Of those that a mesh axis runs over, the one named last changes fastest.
Arguments:
- visibilities: bfloat16 [512, 8, 512], P(('au', 'vert'), None, 'ch'), may hold values from -6 to 6
- tracks: bfloat16 [512, 2, 8], P(('au', 'vert')), may hold values from -10 to 10
- offset_u: int32 [512], P(('au', 'vert')), may hold values from 0 to 255
- offset_v: int32 [512], P(('au', 'vert')), may hold values from 0 to 255
- heading: int32 [512, 1], P(('au', 'vert')), may hold values from 0 to 4; in each aligned block of 32 rows (0 to 31, 32 to 63, ...) at most 8 rows name the same one
- baseline: int32 [512], P(('au', 'vert')), may hold values from 0 to 2015
- station_pair: int32 [2, 2016], replicated, may hold values from 0 to 63, as said below
- screens: bfloat16 [64, 4, 4096], P('ch'), may hold values from -4.1875 to 4.1875
Outputs:
- band_grid: float32 [2, 8, 1024, 1024], P('ch', None, 'au', 'vert')
Inputs may be any that keep to these rules, and one draw needn't show every extreme that they name: Within the blocks of one tile (aligned runs of 32 rows) no heading occurs more than 8 times. `station_pair`: the two stations of a baseline differ.
All inputs are finite; a program needn't handle non-finite values.
Results may differ from a plain program's by a relative error of at most 0.0065.
Values may be sent and summed in bfloat16 or wider, within the bound.
A program may use at most 128 MiB of HBM per device.

v0:
```python
import functools
import math

import jax
import jax.numpy as jnp
import ml_dtypes
import numpy as np
from jax import lax
from jax.experimental import pallas as pl
from jax.experimental.pallas import tpu as pltpu
from jax.sharding import PartitionSpec as P

S = 64
CH_DEV = 32
TB = 8
K = TB * CH_DEV
B_DEV = 32
CAP = B_DEV // 4
SLOTS = 5 * CAP
TU = 256
TV = 256
ROWS = 72
MESH = pl.DeviceIdType.MESH
BF = jnp.bfloat16
F32 = jnp.float32


def series(values, degree):
    nodes = (np.cos(np.pi * (np.arange(400) + 0.5) / 400) + 1.0) * 0.125
    fitted = np.polynomial.chebyshev.Chebyshev.fit(nodes, values(nodes), degree, domain=[0, 0.25])
    return [float(c) for c in fitted.convert(kind=np.polynomial.Polynomial).coef]


COS_COEF = series(lambda q: np.cos(2 * np.pi * np.sqrt(q)), 7)
SIN_COEF = series(lambda q: np.sin(2 * np.pi * np.sqrt(q)) / np.sqrt(q), 6)


def horner(coefs, q):
    total = jnp.full_like(q, coefs[-1])
    for c in coefs[-2::-1]:
        total = total * q + jnp.float32(c)
    return total


def dft_tables():
    centred = np.arange(S) - S // 2
    product = (centred[:, None] * centred[None, :]) % S
    angles = np.float32(2.0 * math.pi / S) * product.astype(np.float32)
    scale = np.float32(1.0 / math.sqrt(S))
    re = (np.cos(angles) * scale).astype(ml_dtypes.bfloat16).astype(np.float32)
    im = (-np.sin(angles) * scale).astype(ml_dtypes.bfloat16).astype(np.float32)
    return re, im


def right_table():
    re, im = dft_tables()
    norm = np.float32(1.0 / math.sqrt(K))
    table = np.zeros((2 * S, 512), np.float32)
    table[:S, :S] = re.T * norm
    table[S:, :S] = -im.T * norm
    table[:S, 256 : 256 + S] = im.T * norm
    table[S:, 256 : 256 + S] = re.T * norm
    return table


def left_table():
    re, im = dft_tables()
    table = np.zeros((8, 2, ROWS, 2 * S), np.float32)
    for shift in range(8):
        table[shift, 0, shift : shift + S, :S] = re
        table[shift, 0, shift : shift + S, S:] = -im
        table[shift, 1, shift : shift + S, :S] = im
        table[shift, 1, shift : shift + S, S:] = re
    return table.reshape(8, 2 * ROWS, 2 * S).astype(ml_dtypes.bfloat16)


def pack_kernel(head, off_u, off_v, base, pairs, data, out_data, out_meta, counts):
    for h in range(5):
        counts[h] = 0
    out_meta[...] = jnp.zeros_like(out_meta)
    lane = lax.broadcasted_iota(jnp.int32, (1, 128), 1)

    def one(b, carry):
        h = head[b]
        slot = h * CAP + counts[h]
        counts[h] = counts[h] + 1
        out_data[slot] = data[b]
        label = base[b]
        row = jnp.where(lane == 0, 1, 0)
        row = jnp.where(lane == 1, off_u[b], row)
        row = jnp.where(lane == 2, off_v[b], row)
        row = jnp.where(lane == 3, pairs[0, label], row)
        row = jnp.where(lane == 4, pairs[1, label], row)
        out_meta[pl.ds(slot, 1), :] = row
        return carry

    lax.fori_loop(0, B_DEV, one, 0)


def exchange_kernel(data, meta, got_data, got_meta, send_sems, recv_sems):
    au, vert = lax.axis_index("au"), lax.axis_index("vert")
    n_au, n_vert = lax.axis_size("au"), lax.axis_size("vert")
    near = (
        {"au": lax.rem(au + 1, n_au)},
        {"au": lax.rem(au + n_au - 1, n_au)},
        {"vert": lax.rem(vert + 1, n_vert)},
        {"vert": lax.rem(vert + n_vert - 1, n_vert)},
    )
    barrier = pltpu.get_barrier_semaphore()
    for device in near:
        pl.semaphore_signal(barrier, inc=1, device_id=device, device_id_type=MESH)
    pl.semaphore_wait(barrier, 4)
    copies = []
    for i, device in enumerate(near):
        for j, (source, target) in enumerate(((data, got_data), (meta, got_meta))):
            copy = pltpu.make_async_remote_copy(
                src_ref=source.at[pl.ds((i + 1) * CAP, CAP)],
                dst_ref=target.at[pl.ds(i * CAP, CAP)],
                send_sem=send_sems.at[i, j],
                recv_sem=recv_sems.at[i, j],
                device_id=device,
                device_id_type=MESH,
            )
            copy.start()
            copies.append(copy)
    for copy in copies:
        copy.wait()


def border_kernel(edge_u, edge_v, corner, got_u, got_v, got_c, send_sems, recv_sems):
    au, vert = lax.axis_index("au"), lax.axis_index("vert")
    n_au, n_vert = lax.axis_size("au"), lax.axis_size("vert")
    au_next, au_last = lax.rem(au + 1, n_au), lax.rem(au + n_au - 1, n_au)
    vert_next, vert_last = lax.rem(vert + 1, n_vert), lax.rem(vert + n_vert - 1, n_vert)
    targets = ({"au": au_next}, {"vert": vert_next}, {"au": au_next, "vert": vert_next})
    sources = ({"au": au_last}, {"vert": vert_last}, {"au": au_last, "vert": vert_last})
    barrier = pltpu.get_barrier_semaphore()
    for device in sources:
        pl.semaphore_signal(barrier, inc=1, device_id=device, device_id_type=MESH)
    pl.semaphore_wait(barrier, 3)
    copies = []
    for i, (source, target) in enumerate(((edge_u, got_u), (edge_v, got_v), (corner, got_c))):
        copy = pltpu.make_async_remote_copy(
            src_ref=source,
            dst_ref=target,
            send_sem=send_sems.at[i],
            recv_sem=recv_sems.at[i],
            device_id=targets[i],
            device_id_type=MESH,
        )
        copy.start()
        copies.append(copy)
    for copy in copies:
        copy.wait()


def swap_halves(x):
    return pltpu.roll(x, S, x.ndim - 1)


def main_kernel(
    own_meta, got_meta, own_data, got_data, own_screens, got_screens, right, left,
    tile, edge_u, edge_v, corner, data, screens, canvas, mult, listing,
):
    band = lax.axis_index("ch")
    channels = CH_DEV * lax.axis_size("ch")
    data[:CAP] = own_data[:CAP]
    data[CAP:] = got_data[...]
    canvas[...] = jnp.zeros_like(canvas)
    row = lax.broadcasted_iota(jnp.int32, (16, K), 0)
    channel = band * CH_DEV + lax.broadcasted_iota(jnp.int32, (16, K), 1) % CH_DEV
    ratio = 1.0 + channel.astype(F32) / jnp.float32(2 * channels)
    step = jnp.where(row < 8, row.astype(F32) / S, (row - 12).astype(F32) / 8)
    mult[...] = step * ratio
    here = own_screens.shape[0]

    def screen_place(station):
        owner = station // here
        local = station - owner * here
        return jnp.where(owner == band, local, here + local)

    def enlist(slot, count):
        own = slot < CAP

        def read(column):
            mine = own_meta[jnp.minimum(slot, CAP - 1), column]
            other = got_meta[jnp.maximum(slot - CAP, 0), column]
            return jnp.where(own, mine, other)

        @pl.when(read(0) == 1)
        def _():
            listing[0, count] = slot
            listing[1, count] = read(1)
            listing[2, count] = read(2)
            listing[3, count] = screen_place(read(3))
            listing[4, count] = screen_place(read(4))

        return count + read(0)

    number = lax.fori_loop(0, SLOTS, enlist, 0)

    copy_own = own_screens
    copy_got = got_screens
    screens[:here] = copy_own[...]
    screens[here:] = copy_got[...]

    def block(index):
        slot = listing[0, index]
        off_u = listing[1, index]
        off_v = listing[2, index]
        one = listing[3, index]
        two = listing[4, index]
        sample = data[slot].astype(F32)
        turns = jnp.concatenate(
            [sample[8:9] * mult[...], sample[9:10] * mult[...]], axis=0
        )
        frac = turns - jnp.floor(turns + 0.5)
        square = frac * frac
        cos = horner(COS_COEF, square)
        sin = horner(SIN_COEF, square) * frac

        def phasors(first):
            cos_fine, sin_fine = cos[first : first + 8], sin[first : first + 8]
            all_cos, all_sin = [], []
            for a in range(8):
                at = first + 8 + a
                cos_a, sin_a = cos[at : at + 1], sin[at : at + 1]
                all_cos.append(cos_fine * cos_a - sin_fine * sin_a)
                all_sin.append(sin_fine * cos_a + cos_fine * sin_a)
            return (
                jnp.concatenate(all_cos, axis=0).astype(BF),
                jnp.concatenate(all_sin, axis=0).astype(BF),
            )

        cos_u, sin_u = phasors(0)
        cos_u, sin_u = cos_u.astype(F32), sin_u.astype(F32)
        cos_v, sin_v = phasors(16)
        table_re = jnp.concatenate([cos_v, sin_v], axis=0)
        table_im = jnp.concatenate([-sin_v, cos_v], axis=0)
        weigh_re, weigh_im = [], []
        for p in range(4):
            re, im = sample[2 * p : 2 * p + 1], sample[2 * p + 1 : 2 * p + 2]
            weigh_re.append((re * cos_u - im * sin_u).astype(BF))
            weigh_im.append((re * sin_u + im * cos_u).astype(BF))
        dims = (((1,), (1,)), ((), ()))
        image = lax.dot_general(
            jnp.concatenate(weigh_re, axis=0), table_re, dims, preferred_element_type=F32
        ) + lax.dot_general(
            jnp.concatenate(weigh_im, axis=0), table_im, dims, preferred_element_type=F32
        )
        two_s = [screens[two, f].astype(F32) for f in range(2)]
        fixed = []
        for f in range(2):
            one_s = screens[one, f].astype(F32)
            one_swapped = swap_halves(one_s)
            for e in range(2):
                p = 2 * f + e
                same = one_s * two_s[e]
                cross = one_swapped * two_s[e]
                gain_re = same + swap_halves(same)
                gain_im = swap_halves(cross) - cross
                part = image[p * S : (p + 1) * S]
                fixed.append((part * gain_re + swap_halves(part) * gain_im).astype(BF))
        lanes = off_v // 128
        shift = off_v - lanes * 128
        shifted = jnp.concatenate(
            [
                pltpu.roll(right[:, :256], shift, 1).astype(BF),
                pltpu.roll(right[:, 256:], shift, 1).astype(BF),
            ],
            axis=1,
        )
        half = jnp.dot(
            jnp.concatenate(fixed, axis=0), shifted, preferred_element_type=F32
        ).astype(BF)
        eighth = off_u // 8
        placed = left[off_u - eighth * 8]
        start_u = pl.multiple_of(eighth * 8, 8)
        start_v = pl.multiple_of(lanes * 128, 128)
        for p in range(4):
            part = half[p * S : (p + 1) * S]
            both = jnp.concatenate([part[:, :256], part[:, 256:]], axis=0)
            grid = jnp.dot(placed, both, preferred_element_type=F32)
            for r in range(2):
                where = (2 * p + r, pl.ds(start_u, ROWS), pl.ds(start_v, 256))
                canvas[where] += grid[r * ROWS : (r + 1) * ROWS]

    def loop(index, carry):
        block(index)
        return carry

    lax.fori_loop(0, number, loop, 0)

    tile[...] = canvas[:, :TU, :TV]
    edge_u[...] = canvas[:, TU:, :TV].astype(BF)
    lane = lax.broadcasted_iota(jnp.int32, (1, 1, 128), 2)

    def folded(x):
        middle = x.shape[1] // 2
        return jnp.where(lane < S, x[:, :middle], swap_halves(x[:, middle:])).astype(BF)

    edge_v[...] = folded(canvas[:, :TU, TV:])
    corner[...] = folded(canvas[:, TU:, TV:])


def finish_kernel(tile, got_u, got_v, got_c, out):
    lane = lax.broadcasted_iota(jnp.int32, (1, 1, 128), 2)

    def unfolded(x):
        x = x.astype(F32)
        low = jnp.where(lane < S, x, 0.0)
        high = jnp.where(lane < S, swap_halves(x), 0.0)
        return jnp.concatenate([low, high], axis=1)

    out[...] = tile[...]
    out[:, :S, :] += got_u[...].astype(F32)
    out[:, :, :128] += unfolded(got_v[...])
    out[:, :S, :128] += unfolded(got_c[...])


def body(visibilities, tracks, offset_u, offset_v, heading, baseline, station_pair, screens):
    smem = pl.BlockSpec(memory_space=pltpu.SMEM)
    vmem = pl.BlockSpec(memory_space=pltpu.VMEM)
    anywhere = pl.BlockSpec(memory_space=pl.ANY)
    n_ch = lax.axis_size("ch")
    here = screens.shape[0]

    arranged = (
        screens.reshape(here, 2, 2, S, S).transpose(0, 1, 3, 2, 4).reshape(here, 2, S, 2 * S)
    )
    other = lax.ppermute(arranged, "ch", [(i, (i + 1) % n_ch) for i in range(n_ch)])

    spread = jnp.broadcast_to(tracks[:, :, :, None], (B_DEV, 2, TB, CH_DEV)).reshape(B_DEV, 2, K)
    data = jnp.concatenate([visibilities, spread, jnp.zeros((B_DEV, 6, K), BF)], axis=1)
    packed, meta = pl.pallas_call(
        pack_kernel,
        out_shape=(
            jax.ShapeDtypeStruct((SLOTS, 16, K), BF),
            jax.ShapeDtypeStruct((SLOTS, 128), jnp.int32),
        ),
        in_specs=[smem] * 5 + [vmem],
        out_specs=(vmem, vmem),
        scratch_shapes=[pltpu.SMEM((8,), jnp.int32)],
    )(heading[:, 0], offset_u, offset_v, baseline, station_pair, data)
    got_data, got_meta = pl.pallas_call(
        exchange_kernel,
        out_shape=(
            jax.ShapeDtypeStruct((SLOTS - CAP, 16, K), BF),
            jax.ShapeDtypeStruct((SLOTS - CAP, 128), jnp.int32),
        ),
        in_specs=[anywhere, anywhere],
        out_specs=(anywhere, anywhere),
        scratch_shapes=[pltpu.SemaphoreType.DMA((4, 2)), pltpu.SemaphoreType.DMA((4, 2))],
        compiler_params=pltpu.CompilerParams(collective_id=0, has_side_effects=True),
    )(packed, meta)
    tile, edge_u, edge_v, corner = pl.pallas_call(
        main_kernel,
        out_shape=(
            jax.ShapeDtypeStruct((8, TU, TV), F32),
            jax.ShapeDtypeStruct((8, S, TV), BF),
            jax.ShapeDtypeStruct((8, TU // 2, 128), BF),
            jax.ShapeDtypeStruct((8, S // 2, 128), BF),
        ),
        in_specs=[smem, smem] + [vmem] * 6,
        out_specs=(vmem,) * 4,
        scratch_shapes=[
            pltpu.VMEM((SLOTS, 16, K), BF),
            pltpu.VMEM((2 * here, 2, S, 2 * S), BF),
            pltpu.VMEM((8, TU + S, TV + 128), F32),
            pltpu.VMEM((16, K), F32),
            pltpu.SMEM((8, SLOTS + 8), jnp.int32),
        ],
        compiler_params=pltpu.CompilerParams(vmem_limit_bytes=40 << 20),
    )(
        meta, got_meta, packed, got_data, arranged, other,
        jnp.asarray(right_table()), jnp.asarray(left_table()),
    )
    got_u, got_v, got_c = pl.pallas_call(
        border_kernel,
        out_shape=(
            jax.ShapeDtypeStruct(edge_u.shape, BF),
            jax.ShapeDtypeStruct(edge_v.shape, BF),
            jax.ShapeDtypeStruct(corner.shape, BF),
        ),
        in_specs=[anywhere] * 3,
        out_specs=(anywhere,) * 3,
        scratch_shapes=[pltpu.SemaphoreType.DMA((3,)), pltpu.SemaphoreType.DMA((3,))],
        compiler_params=pltpu.CompilerParams(collective_id=1, has_side_effects=True),
    )(edge_u, edge_v, corner)
    out = pl.pallas_call(
        finish_kernel,
        out_shape=jax.ShapeDtypeStruct((8, TU, TV), F32),
        in_specs=[vmem] * 4,
        out_specs=vmem,
    )(tile, got_u, got_v, got_c)
    return out[None]


def solution(mesh):
    placed = (
        P(("au", "vert"), None, "ch"),
        P(("au", "vert"), None, None),
        P(("au", "vert")),
        P(("au", "vert")),
        P(("au", "vert"), None),
        P(("au", "vert")),
        P(),
        P("ch", None, None),
    )
    return jax.shard_map(
        body, mesh=mesh, in_specs=placed, out_specs=P("ch", None, "au", "vert"), check_vma=False
    )
```

profile of v0, /device:TPU:0, one launch (start us, length us, event | category | flops | bytes accessed | tf_op | source)
XLA Modules:
  0.0 87.0 jit_solution(4559684499907937513)
XLA Ops:
  0.0 3.3 %reshape.11 = bf16[32,2,2,64,64]{4,3,2,1,0:T(8,128)(2,1)S(1)} reshape(bf16[32,4,4096]{2,1,0:T(4,128)(2,1)} %param.17) | data formatting | bytes 2097152 | tf_op jit(solution)/shard_map/reshape | solution.py:329
  3.3 3.5 %copy.14 = bf16[32,2,2,64,64]{4,2,3,1,0:T(2,128)(2,1)} copy(bf16[32,2,2,64,64]{4,3,2,1,0:T(8,128)(2,1)S(1)} %reshape.11) | data formatting | bytes 2097152 | tf_op jit(solution)/shard_map/reshape | solution.py:329
  6.8 4.0 %reshape.12.own_screens = bf16[32,2,64,128]{3,2,1,0:T(8,128)(2,1)S(1)} reshape(bf16[32,2,64,2,64]{4,3,2,1,0:T(2,128)(2,1)} %bitcast.7) | data formatting | bytes 2097152 | tf_op jit(solution)/shard_map/reshape | solution.py:329
  10.8 3.0 %collective-permute-start = (bf16[32,2,64,128]{3,2,1,0:T(8,128)(2,1)S(1)}, bf16[32,2,64,128]{3,2,1,0:T(8,128)(2,1)S(1)}, u32[]{:S(2)}, u32[]{:S(2)}) collective-permute-start(bf16[32,2,64,128]{3,2,1,0:T(8,128)(2,1)S(1)} %reshape.12.own_screens), channel_id=1, source_target_pairs={{0,1},{1,0},{2,3},{3,2},{4,5},{5,4},{6,7},{7,6},{8,9},{9,8},{10,11... | collective-permute-start | bytes 3145736 | tf_op jit(solution)/shard_map/ppermute | solution.py:331
  13.8 0.1 copy.11
  13.9 0.1 broadcast_in_dim.12
  14.0 0.1 reshape.10
  14.2 0.1 pad.2.clone
  14.2 0.0 copy-done.10
  14.2 0.8 maximum_maximum_fusion.data
  15.0 2.1 %shard_map.100 = (bf16[40,16,256]{2,1,0:T(8,128)(2,1)}, s32[40,128]{1,0:T(8,128)}) custom-call(s32[32]{0:T(128)} %bitcast.8, s32[32]{0:T(128)} %off_u.1, s32[32]{0:T(128)} %off_v.1, s32[32]{0:T(128)} %base.1, s32[2,2016]{1,0:T(2,128)} %pairs.1, bf16[32,16,256]{2,1,0:T(8,128)(2,1)} %maximum_maximum_fusion.data), custom_call_target="tpu_custom_call" | custom-call | tf_op jit(solution)/shard_map/pallas_call | solution.py:335
  17.1 7.6 %shard_map.101 = (bf16[32,16,256]{2,1,0:T(8,128)(2,1)}, s32[32,128]{1,0:T(8,128)}) custom-call(bf16[40,16,256]{2,1,0:T(8,128)(2,1)} %get-tuple-element.17.data.own_data, s32[40,128]{1,0:T(8,128)} %get-tuple-element.16.meta.own_meta), custom_call_target="tpu_custom_call" | custom-call | tf_op jit(solution)/shard_map/pallas_call | solution.py:345
  24.7 12.2 %collective-permute-done.got_screens = bf16[32,2,64,128]{3,2,1,0:T(8,128)(2,1)S(1)} collective-permute-done((bf16[32,2,64,128]{3,2,1,0:T(8,128)(2,1)S(1)}, bf16[32,2,64,128]{3,2,1,0:T(8,128)(2,1)S(1)}, u32[]{:S(2)}, u32[]{:S(2)}) %collective-permute-start) | collective-permute-done | bytes 1048608 | tf_op jit(solution)/shard_map/ppermute | solution.py:331
  37.0 1.0 %copy-done.1 = bf16[40,16,256]{2,1,0:T(8,128)(2,1)S(1)} copy-done((bf16[40,16,256]{2,1,0:T(8,128)(2,1)S(1)}, bf16[40,16,256]{2,1,0:T(8,128)(2,1)}, u32[]{:S(2)}) %copy-start.1) | copy-done | bytes 327704
  37.9 0.9 %copy-done.4 = bf16[32,16,256]{2,1,0:T(8,128)(2,1)S(1)} copy-done((bf16[32,16,256]{2,1,0:T(8,128)(2,1)S(1)}, bf16[32,16,256]{2,1,0:T(8,128)(2,1)}, u32[]{:S(2)}) %copy-start.4) | copy-done | bytes 262168
  38.9 0.7 copy-done.7
  39.6 0.7 copy-done.9
  40.3 27.8 %shard_map.102 = (f32[8,256,256]{2,1,0:T(8,128)S(1)}, bf16[8,64,256]{2,1,0:T(8,128)(2,1)S(1)}, bf16[8,128,128]{2,1,0:T(8,128)(2,1)S(1)}, bf16[8,32,128]{2,1,0:T(8,128)(2,1)S(1)}) custom-call(s32[40,128]{1,0:T(8,128)S(1)} %copy-done.7, s32[32,128]{1,0:T(8,128)S(1)} %copy-done.9, bf16[40,16,256]{2,1,0:T(8,128)(2,1)S(1)} %copy-done.1, ...), custom_call_target="tpu_custom_call" | custom-call | tf_op jit(solution)/shard_map/pallas_call | solution.py:356
  68.1 1.3 %copy-done = f32[8,256,256]{2,1,0:T(8,128)} copy-done((f32[8,256,256]{2,1,0:T(8,128)}, f32[8,256,256]{2,1,0:T(8,128)S(1)}, u32[]{:S(2)}) %copy-start) | copy-done | bytes 2097176
  69.4 0.7 copy-done.5
  70.1 0.7 copy-done.6
  70.9 0.6 copy-done.8
  71.5 12.3 %shard_map.103 = (bf16[8,64,256]{2,1,0:T(8,128)(2,1)}, bf16[8,128,128]{2,1,0:T(8,128)(2,1)}, bf16[8,32,128]{2,1,0:T(8,128)(2,1)}) custom-call(bf16[8,64,256]{2,1,0:T(8,128)(2,1)} %copy-done.5, bf16[8,128,128]{2,1,0:T(8,128)(2,1)} %copy-done.6, bf16[8,32,128]{2,1,0:T(8,128)(2,1)} %copy-done.8), custom_call_target="tpu_custom_call" | custom-call | tf_op jit(solution)/shard_map/pallas_call | solution.py:378
  83.8 3.2 %shard_map.104 = f32[8,256,256]{2,1,0:T(8,128)} custom-call(f32[8,256,256]{2,1,0:T(8,128)} %copy-done, bf16[8,64,256]{2,1,0:T(8,128)(2,1)} %get-tuple-element.24.got_u, bf16[8,128,128]{2,1,0:T(8,128)(2,1)} %get-tuple-element.25.got_v, bf16[8,32,128]{2,1,0:T(8,128)(2,1)} %get-tuple-element.26.got_c), custom_call_target="tpu_custom_call" | custom-call | tf_op jit(solution)/shard_map/pallas_call | solution.py:390
  (16 shorter events, 0.0 us)
Async XLA Ops:
  6.8 7.0 %copy-start.11 = (bf16[32,2,8]{0,2,1:T(8,128)(2,1)S(1)}, bf16[32,2,8]{0,2,1:T(8,128)(2,1)}, u32[]{:S(2)}) copy-start(bf16[32,2,8]{0,2,1:T(8,128)(2,1)} %param.11) | copy-start | bytes 3076
  6.8 7.5 %copy-start.10 = (bf16[32,8,256]{2,1,0:T(8,128)(2,1)S(1)}, bf16[32,8,256]{2,1,0:T(8,128)(2,1)}, u32[]{:S(2)}) copy-start(bf16[32,8,256]{2,1,0:T(8,128)(2,1)} %param.10) | copy-start | bytes 393220
  6.8 30.2 %copy-start.2 = (bf16[8,144,128]{2,1,0:T(8,128)(2,1)S(1)}, bf16[8,144,128]{2,1,0:T(8,128)(2,1)}, u32[]{:S(2)}) copy-start(bf16[8,144,128]{2,1,0:T(8,128)(2,1)} %constant.7.clone.left) | copy-start | bytes 884740
  6.8 30.2 %copy-start.3 = (f32[128,512]{1,0:T(8,128)S(1)}, f32[128,512]{1,0:T(8,128)}, u32[]{:S(2)}) copy-start(f32[128,512]{1,0:T(8,128)} %constant.6.clone.right) | copy-start | bytes 786436
  10.8 26.2 %collective-permute-start = (bf16[32,2,64,128]{3,2,1,0:T(8,128)(2,1)S(1)}, bf16[32,2,64,128]{3,2,1,0:T(8,128)(2,1)S(1)}, u32[]{:S(2)}, u32[]{:S(2)}) collective-permute-start(bf16[32,2,64,128]{3,2,1,0:T(8,128)(2,1)S(1)} %reshape.12.own_screens), channel_id=1, source_target_pairs={{0,1},{1,0},{2,3},{3,2},{4,5},{5,4},{6,7},{7,6},{8,9},{9,8},{10,11... | collective-permute-start | bytes 3145736 | tf_op jit(solution)/shard_map/ppermute | solution.py:331
  37.0 1.0 %copy-start.1 = (bf16[40,16,256]{2,1,0:T(8,128)(2,1)S(1)}, bf16[40,16,256]{2,1,0:T(8,128)(2,1)}, u32[]{:S(2)}) copy-start(bf16[40,16,256]{2,1,0:T(8,128)(2,1)} %get-tuple-element.17.data.own_data) | copy-start | bytes 983044
  37.9 0.9 %copy-start.4 = (bf16[32,16,256]{2,1,0:T(8,128)(2,1)S(1)}, bf16[32,16,256]{2,1,0:T(8,128)(2,1)}, u32[]{:S(2)}) copy-start(bf16[32,16,256]{2,1,0:T(8,128)(2,1)} %get-tuple-element.19.got_data) | copy-start | bytes 786436
  38.9 0.7 copy-start.7
  39.6 0.7 copy-start.9
  68.1 1.3 %copy-start = (f32[8,256,256]{2,1,0:T(8,128)}, f32[8,256,256]{2,1,0:T(8,128)S(1)}, u32[]{:S(2)}) copy-start(f32[8,256,256]{2,1,0:T(8,128)S(1)} %get-tuple-element.20.tile) | copy-start | bytes 6291460
  69.4 0.7 copy-start.5
  70.1 0.7 copy-start.6
  70.9 0.6 copy-start.8
where the time goes:
time: 88.7 us; the launch traced here: 87 us
  Pallas kernels  52.9 us (60%)
  local copies, waits for them, and re-layouts  17.9 us (20%)
  waiting for transfers between devices  12.2 us (14%)
  starting transfers between devices  3.03 us (3%)
    pallas_call x1, Pallas kernels, body(): pl.pallas_call(main_kernel, out_shape=(jax.ShapeDtypeStruct((8, TU, TV),...  27.8 us
    pallas_call x1, Pallas kernels, body(): pl.pallas_call(border_kernel, out_shape=(jax.ShapeDtypeStruct(edge_u.shap...  12.3 us
    ppermute x1, waiting for transfers between devices, body(): lax.ppermute(arranged, 'ch', [(i, (i + 1) % n_ch) for i in range(n_ch)])  12.2 us
    reshape x3, local copies, waits for them, and re-layouts, body(): screens.reshape(here, 2, 2, S, S).transpose(0, 1, 3, 2, 4)  10.7 us
    pallas_call x1, Pallas kernels, body(): pl.pallas_call(exchange_kernel, out_shape=(jax.ShapeDtypeStruct((SLOTS -...  7.59 us
    unnamed x25, local copies, waits for them, and re-layouts  6.86 us
    pallas_call x1, Pallas kernels, body(): pl.pallas_call(finish_kernel, out_shape=jax.ShapeDtypeStruct((8, TU, TV),...  3.23 us
    ppermute x1, starting transfers between devices, body(): lax.ppermute(arranged, 'ch', [(i, (i + 1) % n_ch) for i in range(n_ch)])  3.03 us
  transfers between devices with their start and end apart: 1, of which 1 were waited for; matrix products, arithmetic and copies ran while one was open for 1% of the time, Pallas kernels for 11%

commit v1 on v0

--- a/solution.py
+++ b/solution.py
@@ -65,6 +65,8 @@
 
 def left_table():
     re, im = dft_tables()
+    order = np.concatenate([np.arange(0, S, 2), np.arange(1, S, 2)])
+    re, im = re[:, order], im[:, order]
     table = np.zeros((8, 2, ROWS, 2 * S), np.float32)
     for shift in range(8):
         table[shift, 0, shift : shift + S, :S] = re
@@ -158,61 +160,85 @@
     return pltpu.roll(x, S, x.ndim - 1)
 
 
-def main_kernel(
-    own_meta, got_meta, own_data, got_data, own_screens, got_screens, right, left,
-    tile, edge_u, edge_v, corner, data, screens, canvas, mult, listing,
+def enlist_blocks(own_meta, got_meta, listing):
+    def place(slot, own, read, count):
+        @pl.when(read(0) == 1)
+        def _():
+            listing[0, count] = slot
+            for column in range(1, 5):
+                listing[column, count] = read(column)
+
+        return count + read(0)
+
+    def one_own(slot, count):
+        return place(slot, True, lambda column: own_meta[slot, column], count)
+
+    def one_got(slot, count):
+        return place(slot + CAP, False, lambda column: got_meta[slot, column], count)
+
+    number = lax.fori_loop(0, CAP, one_own, 0)
+    number = lax.fori_loop(0, SLOTS - CAP, one_got, number)
+
+    @pl.when(number % 2 == 1)
+    def _():
+        for column in range(5):
+            listing[column, number] = listing[column, number - 1]
+        listing[1, number] = TU + S
+
+    return (number + 1) // 2
+
+
+def arrange_station(raw, tall):
+    value = raw.astype(F32)
+    for i in range(S // 2):
+        tall[8 * i : 8 * i + 4, :] = value[:, 128 * i : 128 * (i + 1)]
+    lane = lax.broadcasted_iota(jnp.int32, (S // 2, 128), 1)
+    feeds = []
+    for f in range(2):
+        re = tall[pl.ds(2 * f, S // 2, stride=8), :]
+        im = tall[pl.ds(2 * f + 1, S // 2, stride=8), :]
+        even = jnp.where(lane < S, re, swap_halves(im))
+        odd = jnp.where(lane < S, swap_halves(re), im)
+        feeds.append(jnp.concatenate([even, odd], axis=0).astype(BF))
+    return feeds
+
+
+def image_kernel(
+    own_meta_v, got_meta_v, own_data, got_data, own_screens,
+    images, arranged,
+    own_meta, got_meta, data, raw, tall, mult, listing, sems,
 ):
+    fetch = pltpu.make_async_copy(own_screens, raw, sems.at[0])
+    fetch.start()
+    meta_copies = [
+        pltpu.make_async_copy(own_meta_v.at[:CAP], own_meta, sems.at[1]),
+        pltpu.make_async_copy(got_meta_v, got_meta, sems.at[2]),
+    ]
+    for copy in meta_copies:
+        copy.start()
     band = lax.axis_index("ch")
     channels = CH_DEV * lax.axis_size("ch")
     data[:CAP] = own_data[:CAP]
     data[CAP:] = got_data[...]
-    canvas[...] = jnp.zeros_like(canvas)
-    row = lax.broadcasted_iota(jnp.int32, (16, K), 0)
-    channel = band * CH_DEV + lax.broadcasted_iota(jnp.int32, (16, K), 1) % CH_DEV
+    row = lax.broadcasted_iota(jnp.int32, (32, K), 0)
+    channel = band * CH_DEV + lax.broadcasted_iota(jnp.int32, (32, K), 1) % CH_DEV
     ratio = 1.0 + channel.astype(F32) / jnp.float32(2 * channels)
-    step = jnp.where(row < 8, row.astype(F32) / S, (row - 12).astype(F32) / 8)
-    mult[...] = step * ratio
-    here = own_screens.shape[0]
-
-    def screen_place(station):
-        owner = station // here
-        local = station - owner * here
-        return jnp.where(owner == band, local, here + local)
-
-    def enlist(slot, count):
-        own = slot < CAP
-
-        def read(column):
-            mine = own_meta[jnp.minimum(slot, CAP - 1), column]
-            other = got_meta[jnp.maximum(slot - CAP, 0), column]
-            return jnp.where(own, mine, other)
-
-        @pl.when(read(0) == 1)
-        def _():
-            listing[0, count] = slot
-            listing[1, count] = read(1)
-            listing[2, count] = read(2)
-            listing[3, count] = screen_place(read(3))
-            listing[4, count] = screen_place(read(4))
-
-        return count + read(0)
-
-    number = lax.fori_loop(0, SLOTS, enlist, 0)
-
-    copy_own = own_screens
-    copy_got = got_screens
-    screens[:here] = copy_own[...]
-    screens[here:] = copy_got[...]
+    coarse = row - 8
+    coarse_u = 16 * (coarse % 4) + coarse // 4 - S // 2
+    fine_v = row - 16
+    coarse_v = (row - 24) * 8 - S // 2
+    step = jnp.where(
+        row < 16, jnp.where(row < 8, 2 * row, coarse_u), jnp.where(row < 24, fine_v, coarse_v)
+    )
+    mult[...] = step.astype(F32) / S * ratio
+    for copy in meta_copies:
+        copy.wait()
+    pairs = enlist_blocks(own_meta, got_meta, listing)
 
     def block(index):
-        slot = listing[0, index]
-        off_u = listing[1, index]
-        off_v = listing[2, index]
-        one = listing[3, index]
-        two = listing[4, index]
-        sample = data[slot].astype(F32)
+        sample = data[listing[0, index]].astype(F32)
         turns = jnp.concatenate(
-            [sample[8:9] * mult[...], sample[9:10] * mult[...]], axis=0
+            [sample[8:9] * mult[:16], sample[9:10] * mult[16:]], axis=0
         )
         frac = turns - jnp.floor(turns + 0.5)
         square = frac * frac
@@ -248,6 +274,77 @@
         ) + lax.dot_general(
             jnp.concatenate(weigh_im, axis=0), table_im, dims, preferred_element_type=F32
         )
+        return image.astype(BF)
+
+    def loop(pair, carry):
+        first, second = block(2 * pair), block(2 * pair + 1)
+        images[2 * pair] = first
+        images[2 * pair + 1] = second
+        return carry
+
+    lax.fori_loop(0, pairs, loop, 0)
+    fetch.wait()
+
+    def arrange(pair, carry):
+        for i in range(2):
+            feeds = arrange_station(raw[2 * pair + i], tall.at[i])
+            for f in range(2):
+                arranged[2 * pair + i, f] = feeds[f]
+        return carry
+
+    lax.fori_loop(0, raw.shape[0] // 2, arrange, 0)
+
+
+def grid_kernel(
+    own_meta_v, got_meta_v, images, arranged, near_half, far_half, right_in, left_in,
+    tile, edge_u, edge_v, corner,
+    own_meta, got_meta, raw, screens, canvas, right, left, tall, listing, sems,
+):
+    here = arranged.shape[0]
+    part_size = here // 2
+    meta_copies = [
+        pltpu.make_async_copy(own_meta_v.at[:CAP], own_meta, sems.at[0]),
+        pltpu.make_async_copy(got_meta_v, got_meta, sems.at[1]),
+    ]
+    fetches = [
+        pltpu.make_async_copy(near_half, raw.at[:part_size], sems.at[2]),
+        pltpu.make_async_copy(far_half, raw.at[part_size:], sems.at[3]),
+        pltpu.make_async_copy(arranged, screens.at[:here], sems.at[4]),
+        pltpu.make_async_copy(right_in, right, sems.at[5]),
+        pltpu.make_async_copy(left_in, left, sems.at[6]),
+    ]
+    for copy in meta_copies + fetches:
+        copy.start()
+    band = lax.axis_index("ch")
+    parity = lax.rem(lax.axis_index("vert"), 2)
+    canvas[...] = jnp.zeros_like(canvas)
+    for copy in meta_copies:
+        copy.wait()
+    pairs = enlist_blocks(own_meta, got_meta, listing)
+    for copy in fetches:
+        copy.wait()
+
+    def arrange(pair, carry):
+        for i in range(2):
+            feeds = arrange_station(raw[2 * pair + i], tall.at[i])
+            for f in range(2):
+                screens[here + 2 * pair + i, f] = feeds[f]
+        return carry
+
+    lax.fori_loop(0, part_size, arrange, 0)
+
+    def screen_place(station):
+        owner = station // here
+        local = station - owner * here
+        chosen = local // part_size
+        moved = here + local % part_size + jnp.where(chosen == parity, 0, part_size)
+        return jnp.where(owner == band, local, moved)
+
+    def block(index):
+        off_u = listing[1, index]
+        off_v = listing[2, index]
+        one = screen_place(listing[3, index])
+        two = screen_place(listing[4, index])
         two_s = [screens[two, f].astype(F32) for f in range(2)]
         fixed = []
         for f in range(2):
@@ -259,7 +356,7 @@
                 cross = one_swapped * two_s[e]
                 gain_re = same + swap_halves(same)
                 gain_im = swap_halves(cross) - cross
-                part = image[p * S : (p + 1) * S]
+                part = images[index, p * S : (p + 1) * S].astype(F32)
                 fixed.append((part * gain_re + swap_halves(part) * gain_im).astype(BF))
         lanes = off_v // 128
         shift = off_v - lanes * 128
@@ -277,22 +374,26 @@
         placed = left[off_u - eighth * 8]
         start_u = pl.multiple_of(eighth * 8, 8)
         start_v = pl.multiple_of(lanes * 128, 128)
+        grids = []
         for p in range(4):
             part = half[p * S : (p + 1) * S]
             both = jnp.concatenate([part[:, :256], part[:, 256:]], axis=0)
-            grid = jnp.dot(placed, both, preferred_element_type=F32)
-            for r in range(2):
-                where = (2 * p + r, pl.ds(start_u, ROWS), pl.ds(start_v, 256))
-                canvas[where] += grid[r * ROWS : (r + 1) * ROWS]
-
-    def loop(index, carry):
-        block(index)
+            grids.append(jnp.dot(placed, both, preferred_element_type=F32))
+        return start_u, start_v, grids
+
+    def loop(pair, carry):
+        for start_u, start_v, grids in [block(2 * pair), block(2 * pair + 1)]:
+            for p in range(4):
+                for r in range(2):
+                    where = (2 * p + r, pl.ds(start_u, ROWS), pl.ds(start_v, 256))
+                    canvas[where] += grids[p][r * ROWS : (r + 1) * ROWS]
         return carry
 
-    lax.fori_loop(0, number, loop, 0)
-
-    tile[...] = canvas[:, :TU, :TV]
-    edge_u[...] = canvas[:, TU:, :TV].astype(BF)
+    lax.fori_loop(0, pairs, loop, 0)
+
+    store = pltpu.make_async_copy(canvas.at[:, :TU, :TV], tile, sems.at[7])
+    store.start()
+    edge_u[...] = canvas[:, TU : TU + S, :TV].astype(BF)
     lane = lax.broadcasted_iota(jnp.int32, (1, 1, 128), 2)
 
     def folded(x):
@@ -300,22 +401,37 @@
         return jnp.where(lane < S, x[:, :middle], swap_halves(x[:, middle:])).astype(BF)
 
     edge_v[...] = folded(canvas[:, :TU, TV:])
-    corner[...] = folded(canvas[:, TU:, TV:])
-
-
-def finish_kernel(tile, got_u, got_v, got_c, out):
+    corner[...] = folded(canvas[:, TU : TU + S, TV:])
+    store.wait()
+
+
+def finish_kernel(tile, got_u, got_v, got_c, out, top, side, sems):
+    fetch_top = pltpu.make_async_copy(tile.at[:, :S, :], top, sems.at[0])
+    fetch_side = pltpu.make_async_copy(tile.at[:, S:, :128], side, sems.at[1])
+    fetch_top.start()
+    fetch_side.start()
     lane = lax.broadcasted_iota(jnp.int32, (1, 1, 128), 2)
 
     def unfolded(x):
         x = x.astype(F32)
         low = jnp.where(lane < S, x, 0.0)
         high = jnp.where(lane < S, swap_halves(x), 0.0)
-        return jnp.concatenate([low, high], axis=1)
-
-    out[...] = tile[...]
-    out[:, :S, :] += got_u[...].astype(F32)
-    out[:, :, :128] += unfolded(got_v[...])
-    out[:, :S, :128] += unfolded(got_c[...])
+        return low, high
+
+    low, high = unfolded(got_v[...])
+    first, second = unfolded(got_c[...])
+    fetch_top.wait()
+    top[...] += got_u[...].astype(F32)
+    top[:, :, :128] += low[:, :S] + jnp.concatenate([first, second], axis=1)
+    store_top = pltpu.make_async_copy(top, out.at[:, :S, :], sems.at[2])
+    store_top.start()
+    fetch_side.wait()
+    side[:, : TU // 2 - S] += low[:, S:]
+    side[:, TU // 2 - S :] += high
+    store_side = pltpu.make_async_copy(side, out.at[:, S:, :128], sems.at[3])
+    store_side.start()
+    store_top.wait()
+    store_side.wait()
 
 
 def body(visibilities, tracks, offset_u, offset_v, heading, baseline, station_pair, screens):
@@ -325,10 +441,12 @@
     n_ch = lax.axis_size("ch")
     here = screens.shape[0]
 
-    arranged = (
-        screens.reshape(here, 2, 2, S, S).transpose(0, 1, 3, 2, 4).reshape(here, 2, S, 2 * S)
-    )
-    other = lax.ppermute(arranged, "ch", [(i, (i + 1) % n_ch) for i in range(n_ch)])
+    half_size = here // 2
+    n_vert = lax.axis_size("vert")
+    parity = lax.rem(lax.axis_index("vert"), 2)
+    chosen = lax.dynamic_slice_in_dim(screens, parity * half_size, half_size, 0)
+    near_half = lax.ppermute(chosen, "ch", [(i, (i + 1) % n_ch) for i in range(n_ch)])
+    far_half = lax.ppermute(near_half, "vert", [(i, i ^ 1) for i in range(n_vert)])
 
     spread = jnp.broadcast_to(tracks[:, :, :, None], (B_DEV, 2, TB, CH_DEV)).reshape(B_DEV, 2, K)
     data = jnp.concatenate([visibilities, spread, jnp.zeros((B_DEV, 6, K), BF)], axis=1)
@@ -348,31 +466,59 @@
             jax.ShapeDtypeStruct((SLOTS - CAP, 16, K), BF),
             jax.ShapeDtypeStruct((SLOTS - CAP, 128), jnp.int32),
         ),
-        in_specs=[anywhere, anywhere],
-        out_specs=(anywhere, anywhere),
+        in_specs=[vmem, vmem],
+        out_specs=(vmem, vmem),
         scratch_shapes=[pltpu.SemaphoreType.DMA((4, 2)), pltpu.SemaphoreType.DMA((4, 2))],
         compiler_params=pltpu.CompilerParams(collective_id=0, has_side_effects=True),
     )(packed, meta)
+    images, arranged = pl.pallas_call(
+        image_kernel,
+        out_shape=(
+            jax.ShapeDtypeStruct((SLOTS, 4 * S, 2 * S), BF),
+            jax.ShapeDtypeStruct((here, 2, S, 2 * S), BF),
+        ),
+        in_specs=[vmem] * 4 + [anywhere],
+        out_specs=(vmem, vmem),
+        scratch_shapes=[
+            pltpu.SMEM((CAP, 128), jnp.int32),
+            pltpu.SMEM((SLOTS - CAP, 128), jnp.int32),
+            pltpu.VMEM((SLOTS, 16, K), BF),
+            pltpu.VMEM(screens.shape, BF),
+            pltpu.VMEM((2, 4 * S, 128), F32),
+            pltpu.VMEM((32, K), F32),
+            pltpu.SMEM((8, SLOTS + 8), jnp.int32),
+            pltpu.SemaphoreType.DMA((3,)),
+        ],
+        compiler_params=pltpu.CompilerParams(vmem_limit_bytes=20 << 20),
+        cost_estimate=pl.CostEstimate(
+            flops=SLOTS * 2 * 256 * 512 * 128 * 8, bytes_accessed=8 << 20, transcendentals=0
+        ),
+    )(meta, got_meta, packed, got_data, screens)
     tile, edge_u, edge_v, corner = pl.pallas_call(
-        main_kernel,
+        grid_kernel,
         out_shape=(
             jax.ShapeDtypeStruct((8, TU, TV), F32),
             jax.ShapeDtypeStruct((8, S, TV), BF),
             jax.ShapeDtypeStruct((8, TU // 2, 128), BF),
             jax.ShapeDtypeStruct((8, S // 2, 128), BF),
         ),
-        in_specs=[smem, smem] + [vmem] * 6,
-        out_specs=(vmem,) * 4,
+        in_specs=[vmem] * 3 + [anywhere] * 5,
+        out_specs=(anywhere, vmem, vmem, vmem),
         scratch_shapes=[
-            pltpu.VMEM((SLOTS, 16, K), BF),
+            pltpu.SMEM((CAP, 128), jnp.int32),
+            pltpu.SMEM((SLOTS - CAP, 128), jnp.int32),
+            pltpu.VMEM(screens.shape, BF),
             pltpu.VMEM((2 * here, 2, S, 2 * S), BF),
-            pltpu.VMEM((8, TU + S, TV + 128), F32),
-            pltpu.VMEM((16, K), F32),
+            pltpu.VMEM((8, TU + S + ROWS, TV + 128), F32),
+            pltpu.VMEM((2 * S, 512), F32),
+            pltpu.VMEM((8, 2 * ROWS, 2 * S), BF),
+            pltpu.VMEM((2, 4 * S, 128), F32),
             pltpu.SMEM((8, SLOTS + 8), jnp.int32),
+            pltpu.SemaphoreType.DMA((8,)),
         ],
-        compiler_params=pltpu.CompilerParams(vmem_limit_bytes=40 << 20),
+        compiler_params=pltpu.CompilerParams(vmem_limit_bytes=28 << 20),
     )(
-        meta, got_meta, packed, got_data, arranged, other,
+        meta, got_meta, images, arranged, near_half, far_half,
         jnp.asarray(right_table()), jnp.asarray(left_table()),
     )
     got_u, got_v, got_c = pl.pallas_call(
@@ -382,16 +528,22 @@
             jax.ShapeDtypeStruct(edge_v.shape, BF),
             jax.ShapeDtypeStruct(corner.shape, BF),
         ),
-        in_specs=[anywhere] * 3,
-        out_specs=(anywhere,) * 3,
+        in_specs=[vmem] * 3,
+        out_specs=(vmem,) * 3,
         scratch_shapes=[pltpu.SemaphoreType.DMA((3,)), pltpu.SemaphoreType.DMA((3,))],
         compiler_params=pltpu.CompilerParams(collective_id=1, has_side_effects=True),
     )(edge_u, edge_v, corner)
     out = pl.pallas_call(
         finish_kernel,
         out_shape=jax.ShapeDtypeStruct((8, TU, TV), F32),
-        in_specs=[vmem] * 4,
-        out_specs=vmem,
+        in_specs=[anywhere] + [vmem] * 3,
+        out_specs=anywhere,
+        scratch_shapes=[
+            pltpu.VMEM((8, S, TV), F32),
+            pltpu.VMEM((8, TU - S, 128), F32),
+            pltpu.SemaphoreType.DMA((4,)),
+        ],
+        input_output_aliases={0: 0},
     )(tile, got_u, got_v, got_c)
     return out[None]
 

time: 88.7 us -> 71.5 us (0.81); the launches traced: 87 us -> 71.3 us
  waiting for transfers between devices: 12.2 us -> 0.01 us
  local copies, waits for them, and re-layouts: 17.9 us -> 7.8 us
  Pallas kernels: 52.9 us -> 58.3 us
  other arithmetic: 0.8 us -> 1.69 us
    ppermute x1 -> x2, waiting for transfers between devices: 12.2 us -> 0.01 us  [the longest x1 0.01 us: body(): lax.ppermute(chosen, 'ch', [(i, (i + 1) % n_ch) for i in range(n_ch)])]
    reshape x3 -> x0, local copies, waits for them, and re-layouts: 10.7 us -> none  [body(): screens.reshape(here, 2, 2, S, S).transpose(0, 1, 3, 2, 4)]
    pallas_call x1, Pallas kernels: 12.3 us -> 14.3 us  [body(): pl.pallas_call(border_kernel, out_shape=(jax.ShapeDtypeStruct(edge_u.shap...]
    pallas_call x1 -> x2, Pallas kernels: 27.8 us -> 29.6 us  [the longest x1 18.3 us: body(): pl.pallas_call(grid_kernel, out_shape=(jax.ShapeDtypeStruct((8, TU, TV),...]
    pallas_call x1, Pallas kernels: 7.59 us -> 8.95 us  [body(): pl.pallas_call(exchange_kernel, out_shape=(jax.ShapeDtypeStruct((SLOTS -...]
    dynamic_slice x0 -> x1, local copies, waits for them, and re-layouts: none -> 1.32 us  [body(): chosen = lax.dynamic_slice_in_dim(screens, parity * half_size, half_size, 0)]
    concatenate x1, other arithmetic: 0.8 us -> 1.69 us  [body(): jnp.concatenate([visibilities, spread, jnp.zeros((B_DEV, 6, K), BF)], axi...]
    unnamed x25 -> x23, local copies, waits for them, and re-layouts: 6.86 us -> 6.14 us
  transfers between devices with their start and end apart: 1 -> 2, of which waited for: 1 -> 0; matrix products, arithmetic and copies ran while one was open for 1% -> 4% of each run, Pallas kernels for 11% -> 31%
where the time goes in v1:
time: 71.5 us; the launch traced here: 71.3 us
  Pallas kernels  58.3 us (82%)
  local copies, waits for them, and re-layouts  7.8 us (11%)
  starting transfers between devices  3.4 us (5%)
  other arithmetic  1.69 us (2%)
    pallas_call x1, Pallas kernels, body(): pl.pallas_call(grid_kernel, out_shape=(jax.ShapeDtypeStruct((8, TU, TV),...  18.3 us
    pallas_call x1, Pallas kernels, body(): pl.pallas_call(border_kernel, out_shape=(jax.ShapeDtypeStruct(edge_u.shap...  14.3 us
    pallas_call x1, Pallas kernels, body(): pl.pallas_call(image_kernel, out_shape=(jax.ShapeDtypeStruct((SLOTS, 4 *...  11.3 us
    pallas_call x1, Pallas kernels, body(): pl.pallas_call(exchange_kernel, out_shape=(jax.ShapeDtypeStruct((SLOTS -...  8.95 us
    unnamed x23, local copies, waits for them, and re-layouts  6.14 us
    pallas_call x1, Pallas kernels, body(): pl.pallas_call(finish_kernel, out_shape=jax.ShapeDtypeStruct((8, TU, TV),...  3.35 us
    ppermute x1, starting transfers between devices, body(): lax.ppermute(chosen, 'ch', [(i, (i + 1) % n_ch) for i in range(n_ch)])  3.03 us
    pallas_call x1, Pallas kernels, body(): pl.pallas_call(pack_kernel, out_shape=(jax.ShapeDtypeStruct((SLOTS, 16, K...  2.08 us
  transfers between devices with their start and end apart: 2, of which 0 were waited for; matrix products, arithmetic and copies ran while one was open for 4% of the time, Pallas kernels for 31%

profile of v1, /device:TPU:0, one launch (start us, length us, event | category | flops | bytes accessed | tf_op | source)
XLA Modules:
  0.0 71.3 jit_solution(6873518397038226474)
XLA Ops:
  0.0 1.3 %constant_dynamic-slice_fusion = bf16[16,4,4096]{2,1,0:T(4,128)(2,1)S(1)} fusion(bf16[32,4,4096]{2,1,0:T(4,128)(2,1)} %own_screens.1, s32[]{:T(128)S(6)} %select_n.3), kind=kLoop, calls=%fused_computation.1 | loop fusion | bytes 1048580 | tf_op jit(solution)/shard_map/dynamic_slice | solution.py:447
  1.3 3.0 %collective-permute-start = (bf16[16,4,4096]{2,1,0:T(4,128)(2,1)S(1)}, bf16[16,4,4096]{2,1,0:T(4,128)(2,1)S(1)}, u32[]{:S(2)}, u32[]{:S(2)}) collective-permute-start(bf16[16,4,4096]{2,1,0:T(4,128)(2,1)S(1)} %constant_dynamic-slice_fusion), channel_id=1, source_target_pairs={{0,1},{1,0},{2,3},{3,2},{4,5},{5,4},{6,7},{7,6},{8,9},{9,8},{10,11... | collective-permute-start | bytes 1572872 | tf_op jit(solution)/shard_map/ppermute | solution.py:448
  4.4 0.8 %copy.12 = bf16[32,2,8]{2,1,0:T(2,128)(2,1)S(1)} copy(bf16[32,2,8]{0,2,1:T(8,128)(2,1)} %param.11) | data formatting | bytes 2048 | tf_op args[1]
  5.1 0.1 broadcast_in_dim.12
  5.3 0.1 reshape.4
  5.4 0.1 pad.2.clone
  5.5 1.7 %maximum_maximum_fusion.data = bf16[32,16,256]{2,1,0:T(8,128)(2,1)} fusion(bf16[32,2,256]{2,1,0:T(2,128)(2,1)S(1)} %reshape.4, bf16[32,8,256]{2,1,0:T(8,128)(2,1)} %param.10, bf16[16]{0:T(256)(128)(2,1)S(1)} %pad.2.clone), kind=kLoop, calls=%fused_computation | loop fusion | flops 786432 | bytes 426016 | tf_op jit(solution)/shard_map/concatenate | solution.py:452
  7.2 2.1 %shard_map.100 = (bf16[40,16,256]{2,1,0:T(8,128)(2,1)}, s32[40,128]{1,0:T(8,128)}) custom-call(s32[32]{0:T(128)} %bitcast.4, s32[32]{0:T(128)} %off_u.1, s32[32]{0:T(128)} %off_v.1, s32[32]{0:T(128)} %base.1, s32[2,2016]{1,0:T(2,128)} %pairs.1, bf16[32,16,256]{2,1,0:T(8,128)(2,1)} %maximum_maximum_fusion.data), custom_call_target="tpu_custom_call" | custom-call | tf_op jit(solution)/shard_map/pallas_call | solution.py:453
  9.3 8.9 %shard_map.101 = (bf16[32,16,256]{2,1,0:T(8,128)(2,1)}, s32[32,128]{1,0:T(8,128)}) custom-call(bf16[40,16,256]{2,1,0:T(8,128)(2,1)} %get-tuple-element.19.data.own_data, s32[40,128]{1,0:T(8,128)} %get-tuple-element.18.meta.own_meta_v), custom_call_target="tpu_custom_call" | custom-call | tf_op jit(solution)/shard_map/pallas_call | solution.py:463
  18.2 0.0 collective-permute-done.near_half
  18.2 0.4 collective-permute-start.1
  18.6 0.0 copy-done.5
  18.6 1.0 %copy-done = bf16[40,16,256]{2,1,0:T(8,128)(2,1)S(1)} copy-done((bf16[40,16,256]{2,1,0:T(8,128)(2,1)S(1)}, bf16[40,16,256]{2,1,0:T(8,128)(2,1)}, u32[]{:S(2)}) %copy-start) | copy-done | bytes 327704
  19.6 0.7 %copy-done.6 = s32[40,128]{1,0:T(8,128)S(1)} copy-done((s32[40,128]{1,0:T(8,128)S(1)}, s32[40,128]{1,0:T(8,128)}, u32[]{:S(2)}) %copy-start.6) | copy-done | bytes 20504
  20.3 0.7 %copy-done.9 = s32[32,128]{1,0:T(8,128)S(1)} copy-done((s32[32,128]{1,0:T(8,128)S(1)}, s32[32,128]{1,0:T(8,128)}, u32[]{:S(2)}) %copy-start.9) | copy-done | bytes 16408
  21.0 0.9 %copy-done.10 = bf16[32,16,256]{2,1,0:T(8,128)(2,1)S(1)} copy-done((bf16[32,16,256]{2,1,0:T(8,128)(2,1)S(1)}, bf16[32,16,256]{2,1,0:T(8,128)(2,1)}, u32[]{:S(2)}) %copy-start.10) | copy-done | bytes 262168
  22.0 11.3 %shard_map.102 = (bf16[40,256,128]{2,1,0:T(8,128)(2,1)S(1)}, bf16[32,2,64,128]{3,2,1,0:T(8,128)(2,1)S(1)}) custom-call(s32[40,128]{1,0:T(8,128)S(1)} %copy-done.6, s32[32,128]{1,0:T(8,128)S(1)} %copy-done.9, bf16[40,16,256]{2,1,0:T(8,128)(2,1)S(1)} %copy-done, bf16[32,16,256]{2,1,0:T(8,128)(2,1)S(1)} %copy-done.10, bf16[32,4,4096]{2,1,0:T(4,128)(2,1)S(1)} %copy-done.5), custom_call_target="tpu_custom_call" | custom-call | flops 10737418240 | bytes 8388608 | tf_op jit(solution)/shard_map/pallas_call | solution.py:474
  33.3 0.0 collective-permute-done.1.far_half
  33.3 18.3 %shard_map.103 = (f32[8,256,256]{2,1,0:T(8,128)}, bf16[8,64,256]{2,1,0:T(8,128)(2,1)S(1)}, bf16[8,128,128]{2,1,0:T(8,128)(2,1)S(1)}, bf16[8,32,128]{2,1,0:T(8,128)(2,1)S(1)}) custom-call(s32[40,128]{1,0:T(8,128)S(1)} %copy-done.7, s32[32,128]{1,0:T(8,128)S(1)} %copy-done.9, bf16[40,256,128]{2,1,0:T(8,128)(2,1)S(1)} %get-tuple-element.22.images, ...), custom_call_target="tpu_custom_call" | custom-call | tf_op jit(solution)/shard_map/pallas_call | solution.py:497
  51.7 0.7 copy-done.3
  52.3 0.7 copy-done.4
  53.0 0.6 copy-done.8
  53.6 14.3 %shard_map.104 = (bf16[8,64,256]{2,1,0:T(8,128)(2,1)}, bf16[8,128,128]{2,1,0:T(8,128)(2,1)}, bf16[8,32,128]{2,1,0:T(8,128)(2,1)}) custom-call(bf16[8,64,256]{2,1,0:T(8,128)(2,1)} %copy-done.3, bf16[8,128,128]{2,1,0:T(8,128)(2,1)} %copy-done.4, bf16[8,32,128]{2,1,0:T(8,128)(2,1)} %copy-done.8), custom_call_target="tpu_custom_call" | custom-call | tf_op jit(solution)/shard_map/pallas_call | solution.py:524
  68.0 3.3 %shard_map.105 = f32[8,256,256]{2,1,0:T(8,128)} custom-call(f32[8,256,256]{2,1,0:T(8,128)} %get-tuple-element.24.tile, bf16[8,64,256]{2,1,0:T(8,128)(2,1)} %get-tuple-element.28.got_u, bf16[8,128,128]{2,1,0:T(8,128)(2,1)} %get-tuple-element.29.got_v, bf16[8,32,128]{2,1,0:T(8,128)(2,1)} %get-tuple-element.30.got_c), custom_call_target="tpu_custom_call", output_to_operand_aliasing={{}: (0, {})} | custom-call | tf_op jit(solution)/shard_map/pallas_call | solution.py:536
  (15 shorter events, 0.0 us)
Async XLA Ops:
  0.0 18.6 %copy-start.5 = (bf16[32,4,4096]{2,1,0:T(4,128)(2,1)S(1)}, bf16[32,4,4096]{2,1,0:T(4,128)(2,1)}, u32[]{:S(2)}) copy-start(bf16[32,4,4096]{2,1,0:T(4,128)(2,1)} %own_screens.1) | copy-start | bytes 3145732
  1.3 16.9 %collective-permute-start = (bf16[16,4,4096]{2,1,0:T(4,128)(2,1)S(1)}, bf16[16,4,4096]{2,1,0:T(4,128)(2,1)S(1)}, u32[]{:S(2)}, u32[]{:S(2)}) collective-permute-start(bf16[16,4,4096]{2,1,0:T(4,128)(2,1)S(1)} %constant_dynamic-slice_fusion), channel_id=1, source_target_pairs={{0,1},{1,0},{2,3},{3,2},{4,5},{5,4},{6,7},{7,6},{8,9},{9,8},{10,11... | collective-permute-start | bytes 1572872 | tf_op jit(solution)/shard_map/ppermute | solution.py:448
  18.2 15.0 %collective-permute-start.1 = (bf16[16,4,4096]{2,1,0:T(4,128)(2,1)S(1)}, bf16[16,4,4096]{2,1,0:T(4,128)(2,1)S(1)}, u32[]{:S(2)}, u32[]{:S(2)}) collective-permute-start(bf16[16,4,4096]{2,1,0:T(4,128)(2,1)S(1)} %collective-permute-done.near_half), channel_id=1, source_target_pairs={{0,2},{2,0},{4,6},{6,4},{1,3},{3,1},{5,7},{7,5},{8,10},{10,8},{12,... | collective-permute-start | bytes 1572872 | tf_op jit(solution)/shard_map/ppermute | solution.py:449
  18.6 1.0 %copy-start = (bf16[40,16,256]{2,1,0:T(8,128)(2,1)S(1)}, bf16[40,16,256]{2,1,0:T(8,128)(2,1)}, u32[]{:S(2)}) copy-start(bf16[40,16,256]{2,1,0:T(8,128)(2,1)} %get-tuple-element.19.data.own_data) | copy-start | bytes 983044
  19.6 0.7 %copy-start.6 = (s32[40,128]{1,0:T(8,128)S(1)}, s32[40,128]{1,0:T(8,128)}, u32[]{:S(2)}) copy-start(s32[40,128]{1,0:T(8,128)} %get-tuple-element.18.meta.own_meta_v) | copy-start | bytes 61444
  20.3 0.7 %copy-start.9 = (s32[32,128]{1,0:T(8,128)S(1)}, s32[32,128]{1,0:T(8,128)}, u32[]{:S(2)}) copy-start(s32[32,128]{1,0:T(8,128)} %get-tuple-element.20.got_meta_v) | copy-start | bytes 49156
  21.0 0.9 %copy-start.10 = (bf16[32,16,256]{2,1,0:T(8,128)(2,1)S(1)}, bf16[32,16,256]{2,1,0:T(8,128)(2,1)}, u32[]{:S(2)}) copy-start(bf16[32,16,256]{2,1,0:T(8,128)(2,1)} %get-tuple-element.21.got_data) | copy-start | bytes 786436
  22.0 11.3 %copy-start.1 = (bf16[8,144,128]{2,1,0:T(8,128)(2,1)S(1)}, bf16[8,144,128]{2,1,0:T(8,128)(2,1)}, u32[]{:S(2)}) copy-start(bf16[8,144,128]{2,1,0:T(8,128)(2,1)} %constant.23.clone.left_in) | copy-start | bytes 884740
  22.0 11.3 %copy-start.2 = (f32[128,512]{1,0:T(8,128)S(1)}, f32[128,512]{1,0:T(8,128)}, u32[]{:S(2)}) copy-start(f32[128,512]{1,0:T(8,128)} %constant.22.clone.right_in) | copy-start | bytes 786436
  22.0 11.3 %copy-start.7 = (s32[40,128]{1,0:T(8,128)S(1)}, s32[40,128]{1,0:T(8,128)}, u32[]{:S(2)}) copy-start(s32[40,128]{1,0:T(8,128)} %get-tuple-element.18.meta.own_meta_v) | copy-start | bytes 61444
  51.7 0.7 copy-start.3
  52.3 0.7 copy-start.4
  53.0 0.6 copy-start.8

commit v2 on v1

v2 whole, which is shorter than its diff:
```python
import math

import jax
import jax.numpy as jnp
import ml_dtypes
import numpy as np
from jax import lax
from jax.experimental import pallas as pl
from jax.experimental.pallas import tpu as pltpu
from jax.sharding import PartitionSpec as P

S = 64
CH_DEV = 32
TB = 8
K = TB * CH_DEV
B_DEV = 32
CAP = B_DEV // 4
SLOTS = 5 * CAP
TU = 256
TV = 256
ROWS = 72
LATER = 48
MESH = pl.DeviceIdType.MESH
BF = jnp.bfloat16
F32 = jnp.float32


def series(values, degree):
    nodes = (np.cos(np.pi * (np.arange(400) + 0.5) / 400) + 1.0) * 0.125
    fitted = np.polynomial.chebyshev.Chebyshev.fit(nodes, values(nodes), degree, domain=[0, 0.25])
    return [float(c) for c in fitted.convert(kind=np.polynomial.Polynomial).coef]


COS_COEF = series(lambda q: np.cos(2 * np.pi * np.sqrt(q)), 7)
SIN_COEF = series(lambda q: np.sin(2 * np.pi * np.sqrt(q)) / np.sqrt(q), 6)


def horner(coefs, q):
    total = jnp.full_like(q, coefs[-1])
    for c in coefs[-2::-1]:
        total = total * q + jnp.float32(c)
    return total


def dft_tables():
    centred = np.arange(S) - S // 2
    product = (centred[:, None] * centred[None, :]) % S
    angles = np.float32(2.0 * math.pi / S) * product.astype(np.float32)
    scale = np.float32(1.0 / math.sqrt(S))
    re = (np.cos(angles) * scale).astype(ml_dtypes.bfloat16).astype(np.float32)
    im = (-np.sin(angles) * scale).astype(ml_dtypes.bfloat16).astype(np.float32)
    return re, im


def right_table():
    re, im = dft_tables()
    norm = np.float32(1.0 / math.sqrt(K))
    table = np.zeros((2 * S, 512), np.float32)
    table[:S, :S] = re.T * norm
    table[S:, :S] = -im.T * norm
    table[:S, 256 : 256 + S] = im.T * norm
    table[S:, 256 : 256 + S] = re.T * norm
    return table


def left_table():
    re, im = dft_tables()
    order = np.concatenate([np.arange(0, S, 2), np.arange(1, S, 2)])
    re, im = re[:, order], im[:, order]
    table = np.zeros((8, 2, ROWS, 2 * S), np.float32)
    for shift in range(8):
        table[shift, 0, shift : shift + S, :S] = re
        table[shift, 0, shift : shift + S, S:] = -im
        table[shift, 1, shift : shift + S, :S] = im
        table[shift, 1, shift : shift + S, S:] = re
    return table.reshape(8, 2 * ROWS, 2 * S).astype(ml_dtypes.bfloat16)


def pack_kernel(head, off_u, off_v, base, pairs, data, track, out_data, out_meta, rows, counts):
    for h in range(5):
        counts[h] = 0
    out_meta[...] = jnp.zeros_like(out_meta)
    lane = lax.broadcasted_iota(jnp.int32, (TB, 128), 1)
    time = lax.broadcasted_iota(jnp.int32, (TB, 128), 0)
    dims = (((0,), (0,)), ((), ()))
    rows[...] = sum(
        lax.dot_general(
            track[a],
            jnp.where(lane == time + 8 * (a + 1), 1.0, 0.0).astype(BF),
            dims,
            preferred_element_type=F32,
        )
        for a in range(2)
    )
    lane = lax.broadcasted_iota(jnp.int32, (1, 128), 1)

    def one(b, carry):
        h = head[b]
        slot = h * CAP + counts[h]
        counts[h] = counts[h] + 1
        out_data[slot] = data[b]
        label = base[b]
        row = jnp.where(lane == 0, 1, 0)
        row = jnp.where(lane == 1, off_u[b], row)
        row = jnp.where(lane == 2, off_v[b], row)
        row = jnp.where(lane == 3, pairs[0, label], row)
        row = jnp.where(lane == 4, pairs[1, label], row)
        out_meta[pl.ds(slot, 1), :] = rows[pl.ds(b, 1), :] + row.astype(F32)
        return carry

    lax.fori_loop(0, B_DEV, one, 0)


def exchange_kernel(data, meta, got_data, got_meta, send_sems, recv_sems):
    au, vert = lax.axis_index("au"), lax.axis_index("vert")
    n_au, n_vert = lax.axis_size("au"), lax.axis_size("vert")
    near = (
        {"au": lax.rem(au + 1, n_au)},
        {"au": lax.rem(au + n_au - 1, n_au)},
        {"vert": lax.rem(vert + 1, n_vert)},
        {"vert": lax.rem(vert + n_vert - 1, n_vert)},
    )
    barrier = pltpu.get_barrier_semaphore()
    for device in near:
        pl.semaphore_signal(barrier, inc=1, device_id=device, device_id_type=MESH)
    pl.semaphore_wait(barrier, 4)
    copies = []
    for i, device in enumerate(near):
        for j, (source, target) in enumerate(((data, got_data), (meta, got_meta))):
            copy = pltpu.make_async_remote_copy(
                src_ref=source.at[pl.ds((i + 1) * CAP, CAP)],
                dst_ref=target.at[pl.ds(i * CAP, CAP)],
                send_sem=send_sems.at[i, j],
                recv_sem=recv_sems.at[i, j],
                device_id=device,
                device_id_type=MESH,
            )
            copy.start()
            copies.append(copy)
    for copy in copies:
        copy.wait()


def swap_halves(x):
    return pltpu.roll(x, S, x.ndim - 1)


def enlist_blocks(own_meta, got_meta, listing):
    def place(slot, read, counts):
        filled = read(0)
        off_u, off_v = read(1), read(2)
        past = jnp.logical_or(off_u > TU - S, off_v > TV - S)
        index = jnp.where(past, counts[0], LATER + counts[1])

        @pl.when(filled == 1)
        def _():
            listing[0, index] = slot
            listing[1, index] = off_u
            listing[2, index] = off_v
            listing[3, index] = read(3)
            listing[4, index] = read(4)

        early = jnp.where(past, filled, 0)
        return counts[0] + early, counts[1] + filled - early

    def one_own(slot, counts):
        return place(slot, lambda c: own_meta[slot, c].astype(jnp.int32), counts)

    def one_got(slot, counts):
        return place(slot + CAP, lambda c: got_meta[slot, c].astype(jnp.int32), counts)

    counts = (jnp.int32(0), jnp.int32(0))
    counts = lax.fori_loop(0, CAP, one_own, counts)
    counts = lax.fori_loop(0, SLOTS - CAP, one_got, counts)
    for start, number in zip((0, LATER), counts):

        @pl.when(number % 2 == 1)
        def _():
            for column in range(5):
                listing[column, start + number] = listing[column, start + number - 1]
            listing[1, start + number] = TU + S

    return (counts[0] + 1) // 2, (counts[1] + 1) // 2


def arrange_station(raw, tall):
    value = raw.astype(F32)
    for i in range(S // 2):
        tall[8 * i : 8 * i + 4, :] = value[:, 128 * i : 128 * (i + 1)]
    lane = lax.broadcasted_iota(jnp.int32, (S // 2, 128), 1)
    feeds = []
    for f in range(2):
        re = tall[pl.ds(2 * f, S // 2, stride=8), :]
        im = tall[pl.ds(2 * f + 1, S // 2, stride=8), :]
        even = jnp.where(lane < S, re, swap_halves(im))
        odd = jnp.where(lane < S, swap_halves(re), im)
        feeds.append(jnp.concatenate([even, odd], axis=0).astype(BF))
    return feeds


def image_kernel(
    own_meta_in, got_meta_in, own_data, got_data, own_screens,
    images, arranged,
    own_meta, got_meta, data, tracks, spread, raw, tall, mult, listing, sems,
):
    meta_copies = [
        pltpu.make_async_copy(own_meta_in.at[:CAP], own_meta, sems.at[1]),
        pltpu.make_async_copy(got_meta_in, got_meta, sems.at[2]),
        pltpu.make_async_copy(own_meta_in.at[:CAP], tracks.at[:CAP], sems.at[3]),
        pltpu.make_async_copy(got_meta_in, tracks.at[CAP:], sems.at[4]),
    ]
    data_copies = [
        pltpu.make_async_copy(own_data.at[:CAP], data.at[:CAP], sems.at[5]),
        pltpu.make_async_copy(got_data, data.at[CAP:], sems.at[6]),
    ]
    for copy in meta_copies + data_copies:
        copy.start()
    fetch = pltpu.make_async_copy(own_screens, raw, sems.at[0])
    fetch.start()
    band = lax.axis_index("ch")
    channels = CH_DEV * lax.axis_size("ch")
    row = lax.broadcasted_iota(jnp.int32, (32, K), 0)
    channel = band * CH_DEV + lax.broadcasted_iota(jnp.int32, (32, K), 1) % CH_DEV
    ratio = 1.0 + channel.astype(F32) / jnp.float32(2 * channels)
    coarse = row - 8
    coarse_u = 16 * (coarse % 4) + coarse // 4 - S // 2
    fine_v = row - 16
    coarse_v = (row - 24) * 8 - S // 2
    step = jnp.where(
        row < 16, jnp.where(row < 8, 2 * row, coarse_u), jnp.where(row < 24, fine_v, coarse_v)
    )
    mult[...] = step.astype(F32) / S * ratio
    for copy in meta_copies:
        copy.wait()
    source = lax.broadcasted_iota(jnp.int32, (128, 2 * K), 0)
    column = lax.broadcasted_iota(jnp.int32, (128, 2 * K), 1)
    chosen = jnp.where(source == 8 + column // CH_DEV, 1.0, 0.0).astype(BF)
    lane = lax.broadcasted_iota(jnp.int32, (SLOTS, 128), 1)
    only = jnp.where(lane < 8, 0.0, tracks[...]).astype(BF)
    spread[...] = jnp.dot(only, chosen, preferred_element_type=F32)
    early, late = enlist_blocks(own_meta, got_meta, listing)
    for copy in data_copies:
        copy.wait()

    def block(index):
        slot = listing[0, index]
        sample = data[slot].astype(F32)
        track = spread[pl.ds(slot, 1), :]
        turns = jnp.concatenate(
            [track[:, :K] * mult[:16], track[:, K:] * mult[16:]], axis=0
        )
        frac = turns - jnp.floor(turns + 0.5)
        square = frac * frac
        cos = horner(COS_COEF, square)
        sin = horner(SIN_COEF, square) * frac

        def phasors(first):
            cos_fine, sin_fine = cos[first : first + 8], sin[first : first + 8]
            all_cos, all_sin = [], []
            for a in range(8):
                at = first + 8 + a
                cos_a, sin_a = cos[at : at + 1], sin[at : at + 1]
                all_cos.append(cos_fine * cos_a - sin_fine * sin_a)
                all_sin.append(sin_fine * cos_a + cos_fine * sin_a)
            return (
                jnp.concatenate(all_cos, axis=0).astype(BF),
                jnp.concatenate(all_sin, axis=0).astype(BF),
            )

        cos_u, sin_u = phasors(0)
        cos_u, sin_u = cos_u.astype(F32), sin_u.astype(F32)
        cos_v, sin_v = phasors(16)
        table_re = jnp.concatenate([cos_v, sin_v], axis=0)
        table_im = jnp.concatenate([-sin_v, cos_v], axis=0)
        weigh_re, weigh_im = [], []
        for p in range(4):
            re, im = sample[2 * p : 2 * p + 1], sample[2 * p + 1 : 2 * p + 2]
            weigh_re.append((re * cos_u - im * sin_u).astype(BF))
            weigh_im.append((re * sin_u + im * cos_u).astype(BF))
        dims = (((1,), (1,)), ((), ()))
        image = lax.dot_general(
            jnp.concatenate(weigh_re, axis=0), table_re, dims, preferred_element_type=F32
        ) + lax.dot_general(
            jnp.concatenate(weigh_im, axis=0), table_im, dims, preferred_element_type=F32
        )
        return image.astype(BF)

    def loop(pair, carry):
        at = jnp.where(pair < early, 2 * pair, LATER + 2 * (pair - early))
        first, second = block(at), block(at + 1)
        images[2 * pair] = first
        images[2 * pair + 1] = second
        return carry

    lax.fori_loop(0, early + late, loop, 0)
    fetch.wait()

    def arrange(pair, carry):
        for i in range(2):
            feeds = arrange_station(raw[2 * pair + i], tall.at[i])
            for f in range(2):
                arranged[2 * pair + i, f] = feeds[f]
        return carry

    lax.fori_loop(0, raw.shape[0] // 2, arrange, 0)


def folded(x):
    middle = x.shape[1] // 2
    lane = lax.broadcasted_iota(jnp.int32, (1, 1, 128), 2)
    return jnp.where(lane < S, x[:, :middle], swap_halves(x[:, middle:])).astype(BF)


def early_kernel(
    own_meta_in, got_meta_in, images, arranged, got_screens, right_in, left_in,
    canvas, screens, edge_u, edge_v, corner,
    own_meta, got_meta, raw, right, left, tall, listing, sems,
):
    here = arranged.shape[0]
    meta_copies = [
        pltpu.make_async_copy(own_meta_in.at[:CAP], own_meta, sems.at[0]),
        pltpu.make_async_copy(got_meta_in, got_meta, sems.at[1]),
    ]
    fetches = [
        pltpu.make_async_copy(got_screens, raw, sems.at[2]),
        pltpu.make_async_copy(arranged, screens.at[:here], sems.at[3]),
        pltpu.make_async_copy(right_in, right, sems.at[4]),
        pltpu.make_async_copy(left_in, left, sems.at[5]),
    ]
    for copy in meta_copies + fetches:
        copy.start()
    canvas[...] = jnp.zeros_like(canvas)
    for copy in meta_copies:
        copy.wait()
    early, _ = enlist_blocks(own_meta, got_meta, listing)
    for copy in fetches:
        copy.wait()

    def arrange(pair, carry):
        for i in range(2):
            feeds = arrange_station(raw[2 * pair + i], tall.at[i])
            for f in range(2):
                screens[here + 2 * pair + i, f] = feeds[f]
        return carry

    lax.fori_loop(0, here // 2, arrange, 0)
    grid_blocks(images, screens, canvas, right, left, listing, early, 0, 0)
    edge_u[...] = canvas[:, TU : TU + S, :TV].astype(BF)
    edge_v[...] = folded(canvas[:, :TU, TV:])
    corner[...] = folded(canvas[:, TU : TU + S, TV:])


def late_kernel(
    own_meta_in, got_meta_in, images, canvas_in, screens, right_in, left_in,
    canvas, tile,
    own_meta, got_meta, right, left, listing, sems,
):
    meta_copies = [
        pltpu.make_async_copy(own_meta_in.at[:CAP], own_meta, sems.at[0]),
        pltpu.make_async_copy(got_meta_in, got_meta, sems.at[1]),
    ]
    fetches = [
        pltpu.make_async_copy(right_in, right, sems.at[2]),
        pltpu.make_async_copy(left_in, left, sems.at[3]),
    ]
    for copy in meta_copies + fetches:
        copy.start()
    for copy in meta_copies:
        copy.wait()
    early, late = enlist_blocks(own_meta, got_meta, listing)
    for copy in fetches:
        copy.wait()
    grid_blocks(images, screens, canvas, right, left, listing, late, LATER, 2 * early)
    store = pltpu.make_async_copy(canvas.at[:, :TU, :TV], tile, sems.at[4])
    store.start()
    store.wait()


def grid_blocks(images, screens, canvas, right, left, listing, pairs, first, first_image):
    here = screens.shape[0] // 2
    band = lax.axis_index("ch")

    def screen_place(station):
        owner = station // here
        local = station - owner * here
        return jnp.where(owner == band, local, here + local)

    def block(number):
        index = first + number
        off_u = listing[1, index]
        off_v = listing[2, index]
        one = screen_place(listing[3, index])
        two = screen_place(listing[4, index])
        two_s = [screens[two, f].astype(F32) for f in range(2)]
        fixed = []
        for f in range(2):
            one_s = screens[one, f].astype(F32)
            one_swapped = swap_halves(one_s)
            for e in range(2):
                p = 2 * f + e
                same = one_s * two_s[e]
                cross = one_swapped * two_s[e]
                gain_re = same + swap_halves(same)
                gain_im = swap_halves(cross) - cross
                part = images[first_image + number, p * S : (p + 1) * S].astype(F32)
                fixed.append((part * gain_re + swap_halves(part) * gain_im).astype(BF))
        lanes = off_v // 128
        shift = off_v - lanes * 128
        shifted = jnp.concatenate(
            [
                pltpu.roll(right[:, :256], shift, 1).astype(BF),
                pltpu.roll(right[:, 256:], shift, 1).astype(BF),
            ],
            axis=1,
        )
        half = jnp.dot(
            jnp.concatenate(fixed, axis=0), shifted, preferred_element_type=F32
        ).astype(BF)
        eighth = off_u // 8
        placed = left[off_u - eighth * 8]
        start_u = pl.multiple_of(eighth * 8, 8)
        start_v = pl.multiple_of(lanes * 128, 128)
        grids = []
        for p in range(4):
            part = half[p * S : (p + 1) * S]
            both = jnp.concatenate([part[:, :256], part[:, 256:]], axis=0)
            grids.append(jnp.dot(placed, both, preferred_element_type=F32))
        return start_u, start_v, grids

    def loop(pair, carry):
        for start_u, start_v, grids in [block(2 * pair), block(2 * pair + 1)]:
            for p in range(4):
                for r in range(2):
                    where = (2 * p + r, pl.ds(start_u, ROWS), pl.ds(start_v, 256))
                    canvas[where] += grids[p][r * ROWS : (r + 1) * ROWS]
        return carry

    lax.fori_loop(0, pairs, loop, 0)


def finish_kernel(tile, canvas, got_u, got_v, got_c, out, top, side, sems):
    lane = lax.broadcasted_iota(jnp.int32, (1, 1, 128), 2)

    def unfolded(x):
        x = x.astype(F32)
        low = jnp.where(lane < S, x, 0.0)
        high = jnp.where(lane < S, swap_halves(x), 0.0)
        return low, high

    low, high = unfolded(got_v[...])
    first, second = unfolded(got_c[...])
    top[...] = canvas[:, :S, :TV] + got_u[...].astype(F32)
    top[:, :, :128] += low[:, :S] + jnp.concatenate([first, second], axis=1)
    store_top = pltpu.make_async_copy(top, out.at[:, :S, :], sems.at[0])
    store_top.start()
    side[:, : TU // 2 - S] = canvas[:, S : TU // 2, :128] + low[:, S:]
    side[:, TU // 2 - S :] = canvas[:, TU // 2 : TU, :128] + high
    store_side = pltpu.make_async_copy(side, out.at[:, S:, :128], sems.at[1])
    store_side.start()
    store_top.wait()
    store_side.wait()


def body(visibilities, tracks, offset_u, offset_v, heading, baseline, station_pair, screens):
    smem = pl.BlockSpec(memory_space=pltpu.SMEM)
    vmem = pl.BlockSpec(memory_space=pltpu.VMEM)
    anywhere = pl.BlockSpec(memory_space=pl.ANY)
    n_ch, n_au, n_vert = (lax.axis_size(axis) for axis in ("ch", "au", "vert"))
    here = screens.shape[0]
    got_screens = lax.ppermute(screens, "ch", [(i, (i + 1) % n_ch) for i in range(n_ch)])

    packed, meta = pl.pallas_call(
        pack_kernel,
        out_shape=(
            jax.ShapeDtypeStruct((SLOTS, 8, K), BF),
            jax.ShapeDtypeStruct((SLOTS, 128), F32),
        ),
        in_specs=[smem] * 5 + [vmem] * 2,
        out_specs=(vmem, vmem),
        scratch_shapes=[pltpu.VMEM((B_DEV, 128), F32), pltpu.SMEM((8,), jnp.int32)],
    )(
        heading[:, 0], offset_u, offset_v, baseline, station_pair, visibilities,
        tracks.transpose(1, 2, 0),
    )
    got_data, got_meta = pl.pallas_call(
        exchange_kernel,
        out_shape=(
            jax.ShapeDtypeStruct((SLOTS - CAP, 8, K), BF),
            jax.ShapeDtypeStruct((SLOTS - CAP, 128), F32),
        ),
        in_specs=[anywhere, anywhere],
        out_specs=(anywhere, anywhere),
        scratch_shapes=[pltpu.SemaphoreType.DMA((4, 2)), pltpu.SemaphoreType.DMA((4, 2))],
        compiler_params=pltpu.CompilerParams(collective_id=0, has_side_effects=True),
    )(packed, meta)
    meta_scratch = [pltpu.SMEM((CAP, 128), F32), pltpu.SMEM((SLOTS - CAP, 128), F32)]
    listing = pltpu.SMEM((8, 2 * LATER), jnp.int32)
    images, arranged = pl.pallas_call(
        image_kernel,
        out_shape=(
            jax.ShapeDtypeStruct((SLOTS + 2, 4 * S, 2 * S), BF),
            jax.ShapeDtypeStruct((here, 2, S, 2 * S), BF),
        ),
        in_specs=[anywhere] * 5,
        out_specs=(vmem, vmem),
        scratch_shapes=meta_scratch
        + [
            pltpu.VMEM((SLOTS, 8, K), BF),
            pltpu.VMEM((SLOTS, 128), F32),
            pltpu.VMEM((SLOTS, 2 * K), F32),
            pltpu.VMEM(screens.shape, BF),
            pltpu.VMEM((2, 4 * S, 128), F32),
            pltpu.VMEM((32, K), F32),
            listing,
            pltpu.SemaphoreType.DMA((7,)),
        ],
        compiler_params=pltpu.CompilerParams(vmem_limit_bytes=12 << 20),
        cost_estimate=pl.CostEstimate(
            flops=SLOTS * 2 * 256 * 512 * 128 * 8, bytes_accessed=8 << 20, transcendentals=0
        ),
    )(meta, got_meta, packed, got_data, screens)
    right, left = jnp.asarray(right_table()), jnp.asarray(left_table())
    table_scratch = [pltpu.VMEM((2 * S, 512), F32), pltpu.VMEM((8, 2 * ROWS, 2 * S), BF)]
    canvas_shape = jax.ShapeDtypeStruct((8, TU + S + ROWS, TV + 128), F32)
    canvas, all_screens, edge_u, edge_v, corner = pl.pallas_call(
        early_kernel,
        out_shape=(
            canvas_shape,
            jax.ShapeDtypeStruct((2 * here, 2, S, 2 * S), BF),
            jax.ShapeDtypeStruct((8, S, TV), BF),
            jax.ShapeDtypeStruct((8, TU // 2, 128), BF),
            jax.ShapeDtypeStruct((8, S // 2, 128), BF),
        ),
        in_specs=[anywhere] * 2 + [vmem] + [anywhere] * 4,
        out_specs=(vmem,) * 5,
        scratch_shapes=meta_scratch
        + [pltpu.VMEM(screens.shape, BF)]
        + table_scratch
        + [pltpu.VMEM((2, 4 * S, 128), F32), listing, pltpu.SemaphoreType.DMA((6,))],
        compiler_params=pltpu.CompilerParams(vmem_limit_bytes=12 << 20),
    )(meta, got_meta, images, arranged, got_screens, right, left)
    got_u = lax.ppermute(edge_u, "au", [(i, (i + 1) % n_au) for i in range(n_au)])
    got_v = lax.ppermute(edge_v, "vert", [(i, (i + 1) % n_vert) for i in range(n_vert)])
    diagonal = [
        (u * n_vert + v, (u + 1) % n_au * n_vert + (v + 1) % n_vert)
        for u in range(n_au)
        for v in range(n_vert)
    ]
    got_c = lax.ppermute(corner, ("au", "vert"), diagonal)
    canvas, tile = pl.pallas_call(
        late_kernel,
        out_shape=(canvas_shape, jax.ShapeDtypeStruct((8, TU, TV), F32)),
        in_specs=[anywhere] * 2 + [vmem] * 3 + [anywhere] * 2,
        out_specs=(vmem, anywhere),
        scratch_shapes=meta_scratch + table_scratch + [listing, pltpu.SemaphoreType.DMA((5,))],
        input_output_aliases={3: 0},
        compiler_params=pltpu.CompilerParams(vmem_limit_bytes=12 << 20),
        cost_estimate=pl.CostEstimate(
            flops=SLOTS * 2 * 256 * 512 * 128 * 8, bytes_accessed=8 << 20, transcendentals=0
        ),
    )(meta, got_meta, images, canvas, all_screens, right, left)
    out = pl.pallas_call(
        finish_kernel,
        out_shape=jax.ShapeDtypeStruct((8, TU, TV), F32),
        in_specs=[anywhere] + [vmem] * 4,
        out_specs=anywhere,
        scratch_shapes=[
            pltpu.VMEM((8, S, TV), F32),
            pltpu.VMEM((8, TU - S, 128), F32),
            pltpu.SemaphoreType.DMA((2,)),
        ],
        input_output_aliases={0: 0},
        compiler_params=pltpu.CompilerParams(vmem_limit_bytes=8 << 20),
    )(tile, canvas, got_u, got_v, got_c)
    return out[None]


def solution(mesh):
    placed = (
        P(("au", "vert"), None, "ch"),
        P(("au", "vert"), None, None),
        P(("au", "vert")),
        P(("au", "vert")),
        P(("au", "vert"), None),
        P(("au", "vert")),
        P(),
        P("ch", None, None),
    )
    return jax.shard_map(
        body, mesh=mesh, in_specs=placed, out_specs=P("ch", None, "au", "vert"), check_vma=False
    )
```

time: 71.5 us -> 55.6 us (0.78)
  the two profiles are of different devices: /device:TPU:0 before, /device:TPU:17 now
where the time goes in v2:
time: 55.6 us; the launch traced here: 55.2 us
  Pallas kernels  42.1 us (76%)
  starting transfers between devices  8.51 us (15%)
  local copies, waits for them, and re-layouts  4.49 us (8%)
    pallas_call x1, Pallas kernels, body(): pl.pallas_call(late_kernel, out_shape=(canvas_shape, jax.ShapeDtypeStruct...  12 us
    pallas_call x1, Pallas kernels, body(): pl.pallas_call(image_kernel, out_shape=(jax.ShapeDtypeStruct((SLOTS + 2,...  11.7 us
    pallas_call x1, Pallas kernels, body(): pl.pallas_call(early_kernel, out_shape=(canvas_shape, jax.ShapeDtypeStruc...  8.62 us
    ppermute x1, starting transfers between devices, body(): got_c = lax.ppermute(corner, ('au', 'vert'), diagonal)  6.65 us
    pallas_call x1, Pallas kernels, body(): pl.pallas_call(exchange_kernel, out_shape=(jax.ShapeDtypeStruct((SLOTS -...  6.27 us
    unnamed x16, local copies, waits for them, and re-layouts  4.49 us
    pallas_call x1, Pallas kernels, body(): pl.pallas_call(pack_kernel, out_shape=(jax.ShapeDtypeStruct((SLOTS, 8, K)...  2.22 us
    pallas_call x1, Pallas kernels, body(): pl.pallas_call(finish_kernel, out_shape=jax.ShapeDtypeStruct((8, TU, TV),...  1.25 us
  transfers between devices with their start and end apart: 4, of which 0 were waited for; matrix products, arithmetic and copies ran while one was open for 0% of the time, Pallas kernels for 58%

profile of v2, /device:TPU:17, one launch (start us, length us, event | category | flops | bytes accessed | tf_op | source)
XLA Modules:
  0.0 55.2 jit_solution(16211540087106572387)
XLA Ops:
  0.0 1.2 %collective-permute-start = (bf16[32,4,4096]{2,1,0:T(4,128)(2,1)}, bf16[32,4,4096]{2,1,0:T(4,128)(2,1)S(1)}, u32[]{:S(2)}, u32[]{:S(2)}) collective-permute-start(bf16[32,4,4096]{2,1,0:T(4,128)(2,1)} %own_screens.1), channel_id=1, source_target_pairs={{0,1},{1,0},{2,3},{3,2},{4,5},{5,4},{6,7},{7,6},{8,9},{9,8},{10,11... | collective-permute-start | bytes 3145736 | tf_op jit(solution)/shard_map/ppermute | solution.py:470
  1.2 2.2 %shard_map.100 = (bf16[40,8,256]{2,1,0:T(8,128)(2,1)}, f32[40,128]{1,0:T(8,128)}) custom-call(s32[32]{0:T(128)} %bitcast.4, s32[32]{0:T(128)} %off_u.1, s32[32]{0:T(128)} %off_v.1, s32[32]{0:T(128)} %base.1, s32[2,2016]{1,0:T(2,128)} %pairs.1, bf16[32,8,256]{2,1,0:T(8,128)(2,1)} %data.1, bf16[2,8,32]{2,1,0:T(8,128)(2,1)} %bitcast.3), custom_call_target="tpu_custom_call" | custom-call | tf_op jit(solution)/shard_map/pallas_call | solution.py:472
  3.5 6.3 %shard_map.101 = (bf16[32,8,256]{2,1,0:T(8,128)(2,1)}, f32[32,128]{1,0:T(8,128)}) custom-call(bf16[40,8,256]{2,1,0:T(8,128)(2,1)} %get-tuple-element.19.data.own_data, f32[40,128]{1,0:T(8,128)} %get-tuple-element.18.meta.own_meta_in), custom_call_target="tpu_custom_call" | custom-call | tf_op jit(solution)/shard_map/pallas_call | solution.py:485
  9.7 0.0 copy-start.2
  9.7 0.9 %copy-done.2 = bf16[40,8,256]{2,1,0:T(8,128)(2,1)S(1)} copy-done((bf16[40,8,256]{2,1,0:T(8,128)(2,1)S(1)}, bf16[40,8,256]{2,1,0:T(8,128)(2,1)}, u32[]{:S(2)}) %copy-start.2) | copy-done | bytes 163864
  10.7 0.7 %copy-done.3 = f32[40,128]{1,0:T(8,128)S(1)} copy-done((f32[40,128]{1,0:T(8,128)S(1)}, f32[40,128]{1,0:T(8,128)}, u32[]{:S(2)}) %copy-start.3) | copy-done | bytes 20504
  11.4 0.7 %copy-done.5 = f32[32,128]{1,0:T(8,128)S(1)} copy-done((f32[32,128]{1,0:T(8,128)S(1)}, f32[32,128]{1,0:T(8,128)}, u32[]{:S(2)}) %copy-start.5) | copy-done | bytes 16408
  12.1 1.2 %copy-done.6 = bf16[32,4,4096]{2,1,0:T(4,128)(2,1)S(1)} copy-done((bf16[32,4,4096]{2,1,0:T(4,128)(2,1)S(1)}, bf16[32,4,4096]{2,1,0:T(4,128)(2,1)}, u32[]{:S(2)}) %copy-start.6) | copy-done | bytes 1048600
  13.3 0.9 %copy-done.7 = bf16[32,8,256]{2,1,0:T(8,128)(2,1)S(1)} copy-done((bf16[32,8,256]{2,1,0:T(8,128)(2,1)S(1)}, bf16[32,8,256]{2,1,0:T(8,128)(2,1)}, u32[]{:S(2)}) %copy-start.7) | copy-done | bytes 131096
  14.2 11.7 %shard_map.102 = (bf16[42,256,128]{2,1,0:T(8,128)(2,1)S(1)}, bf16[32,2,64,128]{3,2,1,0:T(8,128)(2,1)S(1)}) custom-call(f32[40,128]{1,0:T(8,128)S(1)} %copy-done.3, f32[32,128]{1,0:T(8,128)S(1)} %copy-done.5, bf16[40,8,256]{2,1,0:T(8,128)(2,1)S(1)} %copy-done.2, bf16[32,8,256]{2,1,0:T(8,128)(2,1)S(1)} %copy-done.7, bf16[32,4,4096]{2,1,0:T(4,128)(2,1)S(1)} %copy-done.6), custom_call_target="tpu_custom_call" | custom-call | flops 10737418240 | bytes 8388608 | tf_op jit(solution)/shard_map/pallas_call | solution.py:498
  26.0 0.0 copy-start.4
  26.0 0.0 collective-permute-done.got_screens
  26.0 0.0 copy-done
  26.0 0.0 copy-done.1
  26.0 8.6 %shard_map.103 = (f32[8,392,384]{2,1,0:T(8,128)S(1)}, bf16[64,2,64,128]{3,2,1,0:T(8,128)(2,1)S(1)}, bf16[8,64,256]{2,1,0:T(8,128)(2,1)S(1)}, bf16[8,128,128]{2,1,0:T(8,128)(2,1)S(1)}, bf16[8,32,128]{2,1,0:T(8,128)(2,1)S(1)}) custom-call(f32[40,128]{1,0:T(8,128)S(1)} %copy-done.3, f32[32,128]{1,0:T(8,128)S(1)} %copy-done.5, ...), custom_call_target="tpu_custom_call" | custom-call | tf_op jit(solution)/shard_map/pallas_call | solution.py:525
  34.6 6.6 %collective-permute-start.3 = (bf16[8,32,128]{2,1,0:T(8,128)(2,1)S(1)}, bf16[8,32,128]{2,1,0:T(8,128)(2,1)S(1)}, u32[]{:S(2)}, u32[]{:S(2)}) collective-permute-start(bf16[8,32,128]{2,1,0:T(8,128)(2,1)S(1)} %get-tuple-element.30), channel_id=1, source_target_pairs={{0,10},{2,12},{4,14},{6,8},{8,18},{10,20},{12,22},{14,16},{16,26},... | collective-permute-start | bytes 196616 | tf_op jit(solution)/shard_map/ppermute | solution.py:549
  41.3 0.0 collective-permute-start.1
  41.3 0.6 %collective-permute-start.2 = (bf16[8,128,128]{2,1,0:T(8,128)(2,1)S(1)}, bf16[8,128,128]{2,1,0:T(8,128)(2,1)S(1)}, u32[]{:S(2)}, u32[]{:S(2)}) collective-permute-start(bf16[8,128,128]{2,1,0:T(8,128)(2,1)S(1)} %get-tuple-element.29), channel_id=1, source_target_pairs={{0,2},{2,4},{4,6},{6,0},{1,3},{3,5},{5,7},{7,1},{8,10},{10,12},{12... | collective-permute-start | bytes 786440 | tf_op jit(solution)/shard_map/ppermute | solution.py:543
  41.9 0.0 copy-done.4
  41.9 12.0 %shard_map.104 = (f32[8,392,384]{2,1,0:T(8,128)S(1)}, f32[8,256,256]{2,1,0:T(8,128)}) custom-call(f32[40,128]{1,0:T(8,128)S(1)} %copy-done.4, f32[32,128]{1,0:T(8,128)S(1)} %copy-done.5, bf16[42,256,128]{2,1,0:T(8,128)(2,1)S(1)} %get-tuple-element.22.images, f32[8,392,384]{2,1,0:T(8,128)S(1)} %get-tuple-element.24.canvas_in, ...), custom_call_target="tpu_custom_call", output_to_operand_aliasing={{0}: (3, {})} | custom-call | flops 10737418240 | bytes 8388608 | tf_op jit(solution)/shard_map/pallas_call | solution.py:550
  53.9 0.0 collective-permute-done.3.got_c
  54.0 0.0 collective-permute-done.1.got_u
  54.0 0.0 collective-permute-done.2.got_v
  54.0 1.3 %shard_map.105 = f32[8,256,256]{2,1,0:T(8,128)} custom-call(f32[8,256,256]{2,1,0:T(8,128)} %get-tuple-element.26.tile, f32[8,392,384]{2,1,0:T(8,128)S(1)} %get-tuple-element.27.canvas, bf16[8,64,256]{2,1,0:T(8,128)(2,1)S(1)} %collective-permute-done.1.got_u, bf16[8,128,128]{2,1,0:T(8,128)(2,1)S(1)} %collective-permute-done.2.got_v, ...), custom_call_target="tpu_custom_call", output_to_operand_aliasing={{}: (0, {})} | custom-call | tf_op jit(solution)/shard_map/pallas_call | solution.py:562
  (6 shorter events, 0.0 us)
Async XLA Ops:
  0.0 26.0 %collective-permute-start = (bf16[32,4,4096]{2,1,0:T(4,128)(2,1)}, bf16[32,4,4096]{2,1,0:T(4,128)(2,1)S(1)}, u32[]{:S(2)}, u32[]{:S(2)}) collective-permute-start(bf16[32,4,4096]{2,1,0:T(4,128)(2,1)} %own_screens.1), channel_id=1, source_target_pairs={{0,1},{1,0},{2,3},{3,2},{4,5},{5,4},{6,7},{7,6},{8,9},{9,8},{10,11... | collective-permute-start | bytes 3145736 | tf_op jit(solution)/shard_map/ppermute | solution.py:470
  9.7 0.9 %copy-start.2 = (bf16[40,8,256]{2,1,0:T(8,128)(2,1)S(1)}, bf16[40,8,256]{2,1,0:T(8,128)(2,1)}, u32[]{:S(2)}) copy-start(bf16[40,8,256]{2,1,0:T(8,128)(2,1)} %get-tuple-element.19.data.own_data) | copy-start | bytes 491524
  10.7 0.7 %copy-start.3 = (f32[40,128]{1,0:T(8,128)S(1)}, f32[40,128]{1,0:T(8,128)}, u32[]{:S(2)}) copy-start(f32[40,128]{1,0:T(8,128)} %get-tuple-element.18.meta.own_meta_in) | copy-start | bytes 61444
  11.4 0.7 %copy-start.5 = (f32[32,128]{1,0:T(8,128)S(1)}, f32[32,128]{1,0:T(8,128)}, u32[]{:S(2)}) copy-start(f32[32,128]{1,0:T(8,128)} %get-tuple-element.20.got_meta_in) | copy-start | bytes 49156
  12.1 1.2 %copy-start.6 = (bf16[32,4,4096]{2,1,0:T(4,128)(2,1)S(1)}, bf16[32,4,4096]{2,1,0:T(4,128)(2,1)}, u32[]{:S(2)}) copy-start(bf16[32,4,4096]{2,1,0:T(4,128)(2,1)} %own_screens.1) | copy-start | bytes 3145732
  13.3 0.9 %copy-start.7 = (bf16[32,8,256]{2,1,0:T(8,128)(2,1)S(1)}, bf16[32,8,256]{2,1,0:T(8,128)(2,1)}, u32[]{:S(2)}) copy-start(bf16[32,8,256]{2,1,0:T(8,128)(2,1)} %get-tuple-element.21.got_data) | copy-start | bytes 393220
  14.2 11.8 %copy-start = (bf16[8,144,128]{2,1,0:T(8,128)(2,1)S(1)}, bf16[8,144,128]{2,1,0:T(8,128)(2,1)}, u32[]{:S(2)}) copy-start(bf16[8,144,128]{2,1,0:T(8,128)(2,1)} %constant.5.clone.left_in) | copy-start | bytes 884740
  14.2 11.8 %copy-start.1 = (f32[128,512]{1,0:T(8,128)S(1)}, f32[128,512]{1,0:T(8,128)}, u32[]{:S(2)}) copy-start(f32[128,512]{1,0:T(8,128)} %constant.4.clone.right_in) | copy-start | bytes 786436
  26.0 15.9 %copy-start.4 = (f32[40,128]{1,0:T(8,128)S(1)}, f32[40,128]{1,0:T(8,128)}, u32[]{:S(2)}) copy-start(f32[40,128]{1,0:T(8,128)} %get-tuple-element.18.meta.own_meta_in) | copy-start | bytes 61444
  34.6 19.3 %collective-permute-start.3 = (bf16[8,32,128]{2,1,0:T(8,128)(2,1)S(1)}, bf16[8,32,128]{2,1,0:T(8,128)(2,1)S(1)}, u32[]{:S(2)}, u32[]{:S(2)}) collective-permute-start(bf16[8,32,128]{2,1,0:T(8,128)(2,1)S(1)} %get-tuple-element.30), channel_id=1, source_target_pairs={{0,10},{2,12},{4,14},{6,8},{8,18},{10,20},{12,22},{14,16},{16,26},... | collective-permute-start | bytes 196616 | tf_op jit(solution)/shard_map/ppermute | solution.py:549
  41.3 12.7 %collective-permute-start.1 = (bf16[8,64,256]{2,1,0:T(8,128)(2,1)S(1)}, bf16[8,64,256]{2,1,0:T(8,128)(2,1)S(1)}, u32[]{:S(2)}, u32[]{:S(2)}) collective-permute-start(bf16[8,64,256]{2,1,0:T(8,128)(2,1)S(1)} %get-tuple-element.28), channel_id=1, source_target_pairs={{0,8},{8,16},{16,24},{24,0},{1,9},{9,17},{17,25},{25,1},{2,10},{10... | collective-permute-start | bytes 786440 | tf_op jit(solution)/shard_map/ppermute | solution.py:542
  41.3 12.7 %collective-permute-start.2 = (bf16[8,128,128]{2,1,0:T(8,128)(2,1)S(1)}, bf16[8,128,128]{2,1,0:T(8,128)(2,1)S(1)}, u32[]{:S(2)}, u32[]{:S(2)}) collective-permute-start(bf16[8,128,128]{2,1,0:T(8,128)(2,1)S(1)} %get-tuple-element.29), channel_id=1, source_target_pairs={{0,2},{2,4},{4,6},{6,0},{1,3},{3,5},{5,7},{7,1},{8,10},{10,12},{12... | collective-permute-start | bytes 786440 | tf_op jit(solution)/shard_map/ppermute | solution.py:543

commit v3 on v2

--- a/solution.py
+++ b/solution.py
@@ -55,11 +55,9 @@
 def right_table():
     re, im = dft_tables()
     norm = np.float32(1.0 / math.sqrt(K))
-    table = np.zeros((2 * S, 512), np.float32)
+    table = np.zeros((2 * S, 256), np.float32)
     table[:S, :S] = re.T * norm
-    table[S:, :S] = -im.T * norm
-    table[:S, 256 : 256 + S] = im.T * norm
-    table[S:, 256 : 256 + S] = re.T * norm
+    table[S:, :S] = im.T * norm
     return table
 
 
@@ -111,7 +109,7 @@
     lax.fori_loop(0, B_DEV, one, 0)
 
 
-def exchange_kernel(data, meta, got_data, got_meta, send_sems, recv_sems):
+def exchange_kernel(data, meta, got_data, got_meta, send_sems, recv_sems, own_sems):
     au, vert = lax.axis_index("au"), lax.axis_index("vert")
     n_au, n_vert = lax.axis_size("au"), lax.axis_size("vert")
     near = (
@@ -120,16 +118,22 @@
         {"vert": lax.rem(vert + 1, n_vert)},
         {"vert": lax.rem(vert + n_vert - 1, n_vert)},
     )
+    copies = []
+    for j, (source, target) in enumerate(((data, got_data), (meta, got_meta))):
+        copy = pltpu.make_async_copy(
+            source.at[pl.ds(0, CAP)], target.at[pl.ds(0, CAP)], own_sems.at[j]
+        )
+        copy.start()
+        copies.append(copy)
     barrier = pltpu.get_barrier_semaphore()
     for device in near:
         pl.semaphore_signal(barrier, inc=1, device_id=device, device_id_type=MESH)
     pl.semaphore_wait(barrier, 4)
-    copies = []
     for i, device in enumerate(near):
         for j, (source, target) in enumerate(((data, got_data), (meta, got_meta))):
             copy = pltpu.make_async_remote_copy(
                 src_ref=source.at[pl.ds((i + 1) * CAP, CAP)],
-                dst_ref=target.at[pl.ds(i * CAP, CAP)],
+                dst_ref=target.at[pl.ds((i + 1) * CAP, CAP)],
                 send_sem=send_sems.at[i, j],
                 recv_sem=recv_sems.at[i, j],
                 device_id=device,
@@ -145,7 +149,7 @@
     return pltpu.roll(x, S, x.ndim - 1)
 
 
-def enlist_blocks(own_meta, got_meta, listing):
+def enlist_blocks(labels, listing):
     def place(slot, read, counts):
         filled = read(0)
         off_u, off_v = read(1), read(2)
@@ -163,15 +167,10 @@
         early = jnp.where(past, filled, 0)
         return counts[0] + early, counts[1] + filled - early
 
-    def one_own(slot, counts):
-        return place(slot, lambda c: own_meta[slot, c].astype(jnp.int32), counts)
-
-    def one_got(slot, counts):
-        return place(slot + CAP, lambda c: got_meta[slot, c].astype(jnp.int32), counts)
-
-    counts = (jnp.int32(0), jnp.int32(0))
-    counts = lax.fori_loop(0, CAP, one_own, counts)
-    counts = lax.fori_loop(0, SLOTS - CAP, one_got, counts)
+    def one(slot, counts):
+        return place(slot, lambda c: labels[slot, c].astype(jnp.int32), counts)
+
+    counts = lax.fori_loop(0, SLOTS, one, (jnp.int32(0), jnp.int32(0)))
     for start, number in zip((0, LATER), counts):
 
         @pl.when(number % 2 == 1)
@@ -198,25 +197,9 @@
     return feeds
 
 
-def image_kernel(
-    own_meta_in, got_meta_in, own_data, got_data, own_screens,
-    images, arranged,
-    own_meta, got_meta, data, tracks, spread, raw, tall, mult, listing, sems,
-):
-    meta_copies = [
-        pltpu.make_async_copy(own_meta_in.at[:CAP], own_meta, sems.at[1]),
-        pltpu.make_async_copy(got_meta_in, got_meta, sems.at[2]),
-        pltpu.make_async_copy(own_meta_in.at[:CAP], tracks.at[:CAP], sems.at[3]),
-        pltpu.make_async_copy(got_meta_in, tracks.at[CAP:], sems.at[4]),
-    ]
-    data_copies = [
-        pltpu.make_async_copy(own_data.at[:CAP], data.at[:CAP], sems.at[5]),
-        pltpu.make_async_copy(got_data, data.at[CAP:], sems.at[6]),
-    ]
-    for copy in meta_copies + data_copies:
-        copy.start()
-    fetch = pltpu.make_async_copy(own_screens, raw, sems.at[0])
-    fetch.start()
+def image_kernel(meta, data, images, labels, spread, mult, listing, sems):
+    copy = pltpu.make_async_copy(meta, labels, sems.at[0])
+    copy.start()
     band = lax.axis_index("ch")
     channels = CH_DEV * lax.axis_size("ch")
     row = lax.broadcasted_iota(jnp.int32, (32, K), 0)
@@ -230,17 +213,14 @@
         row < 16, jnp.where(row < 8, 2 * row, coarse_u), jnp.where(row < 24, fine_v, coarse_v)
     )
     mult[...] = step.astype(F32) / S * ratio
-    for copy in meta_copies:
-        copy.wait()
     source = lax.broadcasted_iota(jnp.int32, (128, 2 * K), 0)
     column = lax.broadcasted_iota(jnp.int32, (128, 2 * K), 1)
     chosen = jnp.where(source == 8 + column // CH_DEV, 1.0, 0.0).astype(BF)
     lane = lax.broadcasted_iota(jnp.int32, (SLOTS, 128), 1)
-    only = jnp.where(lane < 8, 0.0, tracks[...]).astype(BF)
+    only = jnp.where(lane < 8, 0.0, meta[...]).astype(BF)
     spread[...] = jnp.dot(only, chosen, preferred_element_type=F32)
-    early, late = enlist_blocks(own_meta, got_meta, listing)
-    for copy in data_copies:
-        copy.wait()
+    copy.wait()
+    early, late = enlist_blocks(labels, listing)
 
     def block(index):
         slot = listing[0, index]
@@ -293,16 +273,6 @@
         return carry
 
     lax.fori_loop(0, early + late, loop, 0)
-    fetch.wait()
-
-    def arrange(pair, carry):
-        for i in range(2):
-            feeds = arrange_station(raw[2 * pair + i], tall.at[i])
-            for f in range(2):
-                arranged[2 * pair + i, f] = feeds[f]
-        return carry
-
-    lax.fori_loop(0, raw.shape[0] // 2, arrange, 0)
 
 
 def folded(x):
@@ -312,27 +282,24 @@
 
 
 def early_kernel(
-    own_meta_in, got_meta_in, images, arranged, got_screens, right_in, left_in,
+    meta, images, own_screens, got_screens, right_in, left_in,
     canvas, screens, edge_u, edge_v, corner,
-    own_meta, got_meta, raw, right, left, tall, listing, sems,
+    labels, raw, right, left, tall, listing, sems,
 ):
-    here = arranged.shape[0]
-    meta_copies = [
-        pltpu.make_async_copy(own_meta_in.at[:CAP], own_meta, sems.at[0]),
-        pltpu.make_async_copy(got_meta_in, got_meta, sems.at[1]),
-    ]
+    here = own_screens.shape[0]
+    meta_copies = [pltpu.make_async_copy(meta, labels, sems.at[0])]
     fetches = [
-        pltpu.make_async_copy(got_screens, raw, sems.at[2]),
-        pltpu.make_async_copy(arranged, screens.at[:here], sems.at[3]),
-        pltpu.make_async_copy(right_in, right, sems.at[4]),
-        pltpu.make_async_copy(left_in, left, sems.at[5]),
+        pltpu.make_async_copy(own_screens, raw.at[:here], sems.at[2]),
+        pltpu.make_async_copy(got_screens, raw.at[here:], sems.at[3]),
+        pltpu.make_async_copy(left_in, left, sems.at[4]),
+        pltpu.make_async_copy(right_in, right, sems.at[5]),
     ]
     for copy in meta_copies + fetches:
         copy.start()
     canvas[...] = jnp.zeros_like(canvas)
     for copy in meta_copies:
         copy.wait()
-    early, _ = enlist_blocks(own_meta, got_meta, listing)
+    early, _ = enlist_blocks(labels, listing)
     for copy in fetches:
         copy.wait()
 
@@ -340,10 +307,10 @@
         for i in range(2):
             feeds = arrange_station(raw[2 * pair + i], tall.at[i])
             for f in range(2):
-                screens[here + 2 * pair + i, f] = feeds[f]
+                screens[2 * pair + i, f] = feeds[f]
         return carry
 
-    lax.fori_loop(0, here // 2, arrange, 0)
+    lax.fori_loop(0, here, arrange, 0)
     grid_blocks(images, screens, canvas, right, left, listing, early, 0, 0)
     edge_u[...] = canvas[:, TU : TU + S, :TV].astype(BF)
     edge_v[...] = folded(canvas[:, :TU, TV:])
@@ -351,32 +318,33 @@
 
 
 def late_kernel(
-    own_meta_in, got_meta_in, images, canvas_in, screens, right_in, left_in,
+    meta, images, canvas_in, screens, right_in, left_in,
     canvas, tile,
-    own_meta, got_meta, right, left, listing, sems,
+    labels, right, left, listing, sems,
 ):
-    meta_copies = [
-        pltpu.make_async_copy(own_meta_in.at[:CAP], own_meta, sems.at[0]),
-        pltpu.make_async_copy(got_meta_in, got_meta, sems.at[1]),
-    ]
+    meta_copies = [pltpu.make_async_copy(meta, labels, sems.at[0])]
     fetches = [
-        pltpu.make_async_copy(right_in, right, sems.at[2]),
-        pltpu.make_async_copy(left_in, left, sems.at[3]),
+        pltpu.make_async_copy(left_in, left, sems.at[2]),
+        pltpu.make_async_copy(right_in, right, sems.at[3]),
     ]
     for copy in meta_copies + fetches:
         copy.start()
     for copy in meta_copies:
         copy.wait()
-    early, late = enlist_blocks(own_meta, got_meta, listing)
+    early, late = enlist_blocks(labels, listing)
     for copy in fetches:
         copy.wait()
-    grid_blocks(images, screens, canvas, right, left, listing, late, LATER, 2 * early)
+    grid_blocks(
+        images, screens, canvas, right, left, listing, late, LATER, 2 * early
+    )
     store = pltpu.make_async_copy(canvas.at[:, :TU, :TV], tile, sems.at[4])
     store.start()
     store.wait()
 
 
-def grid_blocks(images, screens, canvas, right, left, listing, pairs, first, first_image):
+def grid_blocks(
+    images, screens, canvas, right, left, listing, pairs, first, first_image
+):
     here = screens.shape[0] // 2
     band = lax.axis_index("ch")
 
@@ -405,11 +373,12 @@
                 part = images[first_image + number, p * S : (p + 1) * S].astype(F32)
                 fixed.append((part * gain_re + swap_halves(part) * gain_im).astype(BF))
         lanes = off_v // 128
-        shift = off_v - lanes * 128
+        moved = pltpu.roll(right[...], off_v - lanes * 128, 1).astype(BF)
+        table_re, table_im = moved[:S], moved[S:]
         shifted = jnp.concatenate(
             [
-                pltpu.roll(right[:, :256], shift, 1).astype(BF),
-                pltpu.roll(right[:, 256:], shift, 1).astype(BF),
+                jnp.concatenate([table_re, -table_im], axis=0),
+                jnp.concatenate([table_im, table_re], axis=0),
             ],
             axis=1,
         )
@@ -420,19 +389,18 @@
         placed = left[off_u - eighth * 8]
         start_u = pl.multiple_of(eighth * 8, 8)
         start_v = pl.multiple_of(lanes * 128, 128)
-        grids = []
-        for p in range(4):
-            part = half[p * S : (p + 1) * S]
-            both = jnp.concatenate([part[:, :256], part[:, 256:]], axis=0)
-            grids.append(jnp.dot(placed, both, preferred_element_type=F32))
-        return start_u, start_v, grids
+        return start_u, start_v, placed, half
 
     def loop(pair, carry):
-        for start_u, start_v, grids in [block(2 * pair), block(2 * pair + 1)]:
+        ready = [block(2 * pair), block(2 * pair + 1)]
+        for start_u, start_v, placed, half in ready:
             for p in range(4):
+                part = half[p * S : (p + 1) * S]
+                both = jnp.concatenate([part[:, :256], part[:, 256:]], axis=0)
+                grid = jnp.dot(placed, both, preferred_element_type=F32)
                 for r in range(2):
                     where = (2 * p + r, pl.ds(start_u, ROWS), pl.ds(start_v, 256))
-                    canvas[where] += grids[p][r * ROWS : (r + 1) * ROWS]
+                    canvas[where] += grid[r * ROWS : (r + 1) * ROWS]
         return carry
 
     lax.fori_loop(0, pairs, loop, 0)
@@ -485,42 +453,39 @@
     got_data, got_meta = pl.pallas_call(
         exchange_kernel,
         out_shape=(
-            jax.ShapeDtypeStruct((SLOTS - CAP, 8, K), BF),
-            jax.ShapeDtypeStruct((SLOTS - CAP, 128), F32),
+            jax.ShapeDtypeStruct((SLOTS, 8, K), BF),
+            jax.ShapeDtypeStruct((SLOTS, 128), F32),
         ),
         in_specs=[anywhere, anywhere],
         out_specs=(anywhere, anywhere),
-        scratch_shapes=[pltpu.SemaphoreType.DMA((4, 2)), pltpu.SemaphoreType.DMA((4, 2))],
+        scratch_shapes=[
+            pltpu.SemaphoreType.DMA((4, 2)),
+            pltpu.SemaphoreType.DMA((4, 2)),
+            pltpu.SemaphoreType.DMA((2,)),
+        ],
         compiler_params=pltpu.CompilerParams(collective_id=0, has_side_effects=True),
     )(packed, meta)
-    meta_scratch = [pltpu.SMEM((CAP, 128), F32), pltpu.SMEM((SLOTS - CAP, 128), F32)]
+    labels = [pltpu.SMEM((SLOTS, 128), F32)]
     listing = pltpu.SMEM((8, 2 * LATER), jnp.int32)
-    images, arranged = pl.pallas_call(
+    images = pl.pallas_call(
         image_kernel,
-        out_shape=(
-            jax.ShapeDtypeStruct((SLOTS + 2, 4 * S, 2 * S), BF),
-            jax.ShapeDtypeStruct((here, 2, S, 2 * S), BF),
-        ),
-        in_specs=[anywhere] * 5,
-        out_specs=(vmem, vmem),
-        scratch_shapes=meta_scratch
+        out_shape=jax.ShapeDtypeStruct((SLOTS + 2, 4 * S, 2 * S), BF),
+        in_specs=[vmem, vmem],
+        out_specs=vmem,
+        scratch_shapes=labels
         + [
-            pltpu.VMEM((SLOTS, 8, K), BF),
-            pltpu.VMEM((SLOTS, 128), F32),
             pltpu.VMEM((SLOTS, 2 * K), F32),
-            pltpu.VMEM(screens.shape, BF),
-            pltpu.VMEM((2, 4 * S, 128), F32),
             pltpu.VMEM((32, K), F32),
             listing,
-            pltpu.SemaphoreType.DMA((7,)),
+            pltpu.SemaphoreType.DMA((1,)),
         ],
         compiler_params=pltpu.CompilerParams(vmem_limit_bytes=12 << 20),
         cost_estimate=pl.CostEstimate(
             flops=SLOTS * 2 * 256 * 512 * 128 * 8, bytes_accessed=8 << 20, transcendentals=0
         ),
-    )(meta, got_meta, packed, got_data, screens)
+    )(got_meta, got_data)
     right, left = jnp.asarray(right_table()), jnp.asarray(left_table())
-    table_scratch = [pltpu.VMEM((2 * S, 512), F32), pltpu.VMEM((8, 2 * ROWS, 2 * S), BF)]
+    table_scratch = [pltpu.VMEM((2 * S, 256), F32), pltpu.VMEM((8, 2 * ROWS, 2 * S), BF)]
     canvas_shape = jax.ShapeDtypeStruct((8, TU + S + ROWS, TV + 128), F32)
     canvas, all_screens, edge_u, edge_v, corner = pl.pallas_call(
         early_kernel,
@@ -531,14 +496,14 @@
             jax.ShapeDtypeStruct((8, TU // 2, 128), BF),
             jax.ShapeDtypeStruct((8, S // 2, 128), BF),
         ),
-        in_specs=[anywhere] * 2 + [vmem] + [anywhere] * 4,
+        in_specs=[anywhere, vmem] + [anywhere] * 4,
         out_specs=(vmem,) * 5,
-        scratch_shapes=meta_scratch
-        + [pltpu.VMEM(screens.shape, BF)]
+        scratch_shapes=labels
+        + [pltpu.VMEM((2 * here, 4, S * S), BF)]
         + table_scratch
         + [pltpu.VMEM((2, 4 * S, 128), F32), listing, pltpu.SemaphoreType.DMA((6,))],
         compiler_params=pltpu.CompilerParams(vmem_limit_bytes=12 << 20),
-    )(meta, got_meta, images, arranged, got_screens, right, left)
+    )(got_meta, images, screens, got_screens, right, left)
     got_u = lax.ppermute(edge_u, "au", [(i, (i + 1) % n_au) for i in range(n_au)])
     got_v = lax.ppermute(edge_v, "vert", [(i, (i + 1) % n_vert) for i in range(n_vert)])
     diagonal = [
@@ -550,15 +515,15 @@
     canvas, tile = pl.pallas_call(
         late_kernel,
         out_shape=(canvas_shape, jax.ShapeDtypeStruct((8, TU, TV), F32)),
-        in_specs=[anywhere] * 2 + [vmem] * 3 + [anywhere] * 2,
+        in_specs=[anywhere] + [vmem] * 3 + [anywhere] * 2,
         out_specs=(vmem, anywhere),
-        scratch_shapes=meta_scratch + table_scratch + [listing, pltpu.SemaphoreType.DMA((5,))],
-        input_output_aliases={3: 0},
+        scratch_shapes=labels + table_scratch + [listing, pltpu.SemaphoreType.DMA((6,))],
+        input_output_aliases={2: 0},
         compiler_params=pltpu.CompilerParams(vmem_limit_bytes=12 << 20),
         cost_estimate=pl.CostEstimate(
             flops=SLOTS * 2 * 256 * 512 * 128 * 8, bytes_accessed=8 << 20, transcendentals=0
         ),
-    )(meta, got_meta, images, canvas, all_screens, right, left)
+    )(got_meta, images, canvas, all_screens, right, left)
     out = pl.pallas_call(
         finish_kernel,
         out_shape=jax.ShapeDtypeStruct((8, TU, TV), F32),

time: 55.6 us -> 52.5 us (0.944)
  the two profiles are of different devices: /device:TPU:17 before, /device:TPU:1 now
where the time goes in v3:
time: 52.5 us; the launch traced here: 52.8 us
  Pallas kernels  42 us (80%)
  starting transfers between devices  7.61 us (14%)
  local copies, waits for them, and re-layouts  1.65 us (3%)
  waiting for transfers between devices  1.45 us (3%)
    pallas_call x1, Pallas kernels, body(): pl.pallas_call(late_kernel, out_shape=(canvas_shape, jax.ShapeDtypeStruct...  11 us
    pallas_call x1, Pallas kernels, body(): pl.pallas_call(early_kernel, out_shape=(canvas_shape, jax.ShapeDtypeStruc...  9.8 us
    pallas_call x1, Pallas kernels, body(): pl.pallas_call(image_kernel, out_shape=jax.ShapeDtypeStruct((SLOTS + 2, 4...  9.79 us
    pallas_call x1, Pallas kernels, body(): pl.pallas_call(exchange_kernel, out_shape=(jax.ShapeDtypeStruct((SLOTS, 8...  7.96 us
    ppermute x1, starting transfers between devices, body(): got_c = lax.ppermute(corner, ('au', 'vert'), diagonal)  4.37 us
    pallas_call x1, Pallas kernels, body(): pl.pallas_call(pack_kernel, out_shape=(jax.ShapeDtypeStruct((SLOTS, 8, K)...  2.22 us
    ppermute x1, starting transfers between devices, body(): lax.ppermute(screens, 'ch', [(i, (i + 1) % n_ch) for i in range(n_ch)])  2.07 us
    unnamed x12, local copies, waits for them, and re-layouts  1.65 us
  transfers between devices with their start and end apart: 4, of which 1 were waited for; matrix products, arithmetic and copies ran while one was open for 0% of the time, Pallas kernels for 59%

profile of v3, /device:TPU:1, one launch (start us, length us, event | category | flops | bytes accessed | tf_op | source)
XLA Modules:
  0.0 52.8 jit_solution(7174214315569842089)
XLA Ops:
  0.0 2.1 %collective-permute-start = (bf16[32,4,4096]{2,1,0:T(4,128)(2,1)}, bf16[32,4,4096]{2,1,0:T(4,128)(2,1)S(1)}, u32[]{:S(2)}, u32[]{:S(2)}) collective-permute-start(bf16[32,4,4096]{2,1,0:T(4,128)(2,1)} %own_screens.1), channel_id=1, source_target_pairs={{0,1},{1,0},{2,3},{3,2},{4,5},{5,4},{6,7},{7,6},{8,9},{9,8},{10,11... | collective-permute-start | bytes 3145736 | tf_op jit(solution)/shard_map/ppermute | solution.py:438
  2.1 2.2 %shard_map.100 = (bf16[40,8,256]{2,1,0:T(8,128)(2,1)}, f32[40,128]{1,0:T(8,128)}) custom-call(s32[32]{0:T(128)} %bitcast.4, s32[32]{0:T(128)} %off_u.1, s32[32]{0:T(128)} %off_v.1, s32[32]{0:T(128)} %base.1, s32[2,2016]{1,0:T(2,128)} %pairs.1, bf16[32,8,256]{2,1,0:T(8,128)(2,1)} %data.1, bf16[2,8,32]{2,1,0:T(8,128)(2,1)} %bitcast.3), custom_call_target="tpu_custom_call" | custom-call | tf_op jit(solution)/shard_map/pallas_call | solution.py:440
  4.3 8.0 %shard_map.101 = (bf16[40,8,256]{2,1,0:T(8,128)(2,1)}, f32[40,128]{1,0:T(8,128)}) custom-call(bf16[40,8,256]{2,1,0:T(8,128)(2,1)} %get-tuple-element.16.data, f32[40,128]{1,0:T(8,128)} %get-tuple-element.17.meta), custom_call_target="tpu_custom_call" | custom-call | tf_op jit(solution)/shard_map/pallas_call | solution.py:453
  12.3 0.0 copy-start.3
  12.3 0.7 %copy-done.3 = f32[40,128]{1,0:T(8,128)S(1)} copy-done((f32[40,128]{1,0:T(8,128)S(1)}, f32[40,128]{1,0:T(8,128)}, u32[]{:S(2)}) %copy-start.3) | copy-done | bytes 20504
  13.0 0.0 copy-start.5
  13.0 0.9 %copy-done.5 = bf16[40,8,256]{2,1,0:T(8,128)(2,1)S(1)} copy-done((bf16[40,8,256]{2,1,0:T(8,128)(2,1)S(1)}, bf16[40,8,256]{2,1,0:T(8,128)(2,1)}, u32[]{:S(2)}) %copy-start.5) | copy-done | bytes 163864
  13.9 0.0 copy-start
  13.9 9.8 %shard_map.102.images = bf16[42,256,128]{2,1,0:T(8,128)(2,1)S(1)} custom-call(f32[40,128]{1,0:T(8,128)S(1)} %copy-done.3, bf16[40,8,256]{2,1,0:T(8,128)(2,1)S(1)} %copy-done.5), custom_call_target="tpu_custom_call" | custom-call | flops 10737418240 | bytes 8388608 | tf_op jit(solution)/shard_map/pallas_call | solution.py:470
  23.7 0.0 copy-start.4
  23.7 1.4 %collective-permute-done.got_screens = bf16[32,4,4096]{2,1,0:T(4,128)(2,1)S(1)} collective-permute-done((bf16[32,4,4096]{2,1,0:T(4,128)(2,1)}, bf16[32,4,4096]{2,1,0:T(4,128)(2,1)S(1)}, u32[]{:S(2)}, u32[]{:S(2)}) %collective-permute-start) | collective-permute-done | bytes 1048608 | tf_op jit(solution)/shard_map/ppermute | solution.py:438
  25.2 0.0 copy-done
  25.2 0.0 copy-done.1
  25.2 0.0 copy-done.2
  25.2 9.8 %shard_map.103 = (f32[8,392,384]{2,1,0:T(8,128)S(1)}, bf16[64,2,64,128]{3,2,1,0:T(8,128)(2,1)S(1)}, bf16[8,64,256]{2,1,0:T(8,128)(2,1)S(1)}, bf16[8,128,128]{2,1,0:T(8,128)(2,1)S(1)}, bf16[8,32,128]{2,1,0:T(8,128)(2,1)S(1)}) custom-call(f32[40,128]{1,0:T(8,128)S(1)} %copy-done.3, bf16[42,256,128]{2,1,0:T(8,128)(2,1)S(1)} %shard_map.102.images, ...), custom_call_target="tpu_custom_call" | custom-call | tf_op jit(solution)/shard_map/pallas_call | solution.py:490
  35.0 4.4 %collective-permute-start.3 = (bf16[8,32,128]{2,1,0:T(8,128)(2,1)S(1)}, bf16[8,32,128]{2,1,0:T(8,128)(2,1)S(1)}, u32[]{:S(2)}, u32[]{:S(2)}) collective-permute-start(bf16[8,32,128]{2,1,0:T(8,128)(2,1)S(1)} %get-tuple-element.26), channel_id=1, source_target_pairs={{0,10},{2,12},{4,14},{6,8},{8,18},{10,20},{12,22},{14,16},{16,26},... | collective-permute-start | bytes 196616 | tf_op jit(solution)/shard_map/ppermute | solution.py:514
  39.3 0.6 %collective-permute-start.1 = (bf16[8,64,256]{2,1,0:T(8,128)(2,1)S(1)}, bf16[8,64,256]{2,1,0:T(8,128)(2,1)S(1)}, u32[]{:S(2)}, u32[]{:S(2)}) collective-permute-start(bf16[8,64,256]{2,1,0:T(8,128)(2,1)S(1)} %get-tuple-element.24), channel_id=1, source_target_pairs={{0,8},{8,16},{16,24},{24,0},{1,9},{9,17},{17,25},{25,1},{2,10},{10... | collective-permute-start | bytes 786440 | tf_op jit(solution)/shard_map/ppermute | solution.py:507
  39.9 0.6 %collective-permute-start.2 = (bf16[8,128,128]{2,1,0:T(8,128)(2,1)S(1)}, bf16[8,128,128]{2,1,0:T(8,128)(2,1)S(1)}, u32[]{:S(2)}, u32[]{:S(2)}) collective-permute-start(bf16[8,128,128]{2,1,0:T(8,128)(2,1)S(1)} %get-tuple-element.25), channel_id=1, source_target_pairs={{0,2},{2,4},{4,6},{6,0},{1,3},{3,5},{5,7},{7,1},{8,10},{10,12},{12... | collective-permute-start | bytes 786440 | tf_op jit(solution)/shard_map/ppermute | solution.py:508
  40.5 0.0 copy-done.4
  40.5 11.0 %shard_map.104 = (f32[8,392,384]{2,1,0:T(8,128)S(1)}, f32[8,256,256]{2,1,0:T(8,128)}) custom-call(f32[40,128]{1,0:T(8,128)S(1)} %copy-done.4, bf16[42,256,128]{2,1,0:T(8,128)(2,1)S(1)} %shard_map.102.images, f32[8,392,384]{2,1,0:T(8,128)S(1)} %get-tuple-element.20.canvas_in, ...), custom_call_target="tpu_custom_call", output_to_operand_aliasing={{0}: (2, {})} | custom-call | flops 10737418240 | bytes 8388608 | tf_op jit(solution)/shard_map/pallas_call | solution.py:515
  51.5 0.0 collective-permute-done.3.got_c
  51.5 0.0 collective-permute-done.1.got_u
  51.5 0.0 collective-permute-done.2.got_v
  51.5 1.3 %shard_map.105 = f32[8,256,256]{2,1,0:T(8,128)} custom-call(f32[8,256,256]{2,1,0:T(8,128)} %get-tuple-element.22.tile, f32[8,392,384]{2,1,0:T(8,128)S(1)} %get-tuple-element.23.canvas, bf16[8,64,256]{2,1,0:T(8,128)(2,1)S(1)} %collective-permute-done.1.got_u, bf16[8,128,128]{2,1,0:T(8,128)(2,1)S(1)} %collective-permute-done.2.got_v, ...), custom_call_target="tpu_custom_call", output_to_operand_aliasing={{}: (0, {})} | custom-call | tf_op jit(solution)/shard_map/pallas_call | solution.py:527
  (2 shorter events, 0.0 us)
Async XLA Ops:
  0.0 25.2 %collective-permute-start = (bf16[32,4,4096]{2,1,0:T(4,128)(2,1)}, bf16[32,4,4096]{2,1,0:T(4,128)(2,1)S(1)}, u32[]{:S(2)}, u32[]{:S(2)}) collective-permute-start(bf16[32,4,4096]{2,1,0:T(4,128)(2,1)} %own_screens.1), channel_id=1, source_target_pairs={{0,1},{1,0},{2,3},{3,2},{4,5},{5,4},{6,7},{7,6},{8,9},{9,8},{10,11... | collective-permute-start | bytes 3145736 | tf_op jit(solution)/shard_map/ppermute | solution.py:438
  12.3 0.7 %copy-start.3 = (f32[40,128]{1,0:T(8,128)S(1)}, f32[40,128]{1,0:T(8,128)}, u32[]{:S(2)}) copy-start(f32[40,128]{1,0:T(8,128)} %get-tuple-element.18.meta) | copy-start | bytes 61444
  13.0 0.9 %copy-start.5 = (bf16[40,8,256]{2,1,0:T(8,128)(2,1)S(1)}, bf16[40,8,256]{2,1,0:T(8,128)(2,1)}, u32[]{:S(2)}) copy-start(bf16[40,8,256]{2,1,0:T(8,128)(2,1)} %get-tuple-element.19.data) | copy-start | bytes 491524
  13.9 11.3 %copy-start = (bf16[32,4,4096]{2,1,0:T(4,128)(2,1)S(1)}, bf16[32,4,4096]{2,1,0:T(4,128)(2,1)}, u32[]{:S(2)}) copy-start(bf16[32,4,4096]{2,1,0:T(4,128)(2,1)} %own_screens.1) | copy-start | bytes 3145732
  13.9 11.3 %copy-start.1 = (bf16[8,144,128]{2,1,0:T(8,128)(2,1)S(1)}, bf16[8,144,128]{2,1,0:T(8,128)(2,1)}, u32[]{:S(2)}) copy-start(bf16[8,144,128]{2,1,0:T(8,128)(2,1)} %constant.5.clone.left_in) | copy-start | bytes 884740
  13.9 11.3 %copy-start.2 = (f32[128,256]{1,0:T(8,128)S(1)}, f32[128,256]{1,0:T(8,128)}, u32[]{:S(2)}) copy-start(f32[128,256]{1,0:T(8,128)} %constant.4.clone.right_in) | copy-start | bytes 393220
  23.7 16.8 %copy-start.4 = (f32[40,128]{1,0:T(8,128)S(1)}, f32[40,128]{1,0:T(8,128)}, u32[]{:S(2)}) copy-start(f32[40,128]{1,0:T(8,128)} %get-tuple-element.18.meta) | copy-start | bytes 61444
  35.0 16.5 %collective-permute-start.3 = (bf16[8,32,128]{2,1,0:T(8,128)(2,1)S(1)}, bf16[8,32,128]{2,1,0:T(8,128)(2,1)S(1)}, u32[]{:S(2)}, u32[]{:S(2)}) collective-permute-start(bf16[8,32,128]{2,1,0:T(8,128)(2,1)S(1)} %get-tuple-element.26), channel_id=1, source_target_pairs={{0,10},{2,12},{4,14},{6,8},{8,18},{10,20},{12,22},{14,16},{16,26},... | collective-permute-start | bytes 196616 | tf_op jit(solution)/shard_map/ppermute | solution.py:514
  39.3 12.2 %collective-permute-start.1 = (bf16[8,64,256]{2,1,0:T(8,128)(2,1)S(1)}, bf16[8,64,256]{2,1,0:T(8,128)(2,1)S(1)}, u32[]{:S(2)}, u32[]{:S(2)}) collective-permute-start(bf16[8,64,256]{2,1,0:T(8,128)(2,1)S(1)} %get-tuple-element.24), channel_id=1, source_target_pairs={{0,8},{8,16},{16,24},{24,0},{1,9},{9,17},{17,25},{25,1},{2,10},{10... | collective-permute-start | bytes 786440 | tf_op jit(solution)/shard_map/ppermute | solution.py:507
  39.9 11.6 %collective-permute-start.2 = (bf16[8,128,128]{2,1,0:T(8,128)(2,1)S(1)}, bf16[8,128,128]{2,1,0:T(8,128)(2,1)S(1)}, u32[]{:S(2)}, u32[]{:S(2)}) collective-permute-start(bf16[8,128,128]{2,1,0:T(8,128)(2,1)S(1)} %get-tuple-element.25), channel_id=1, source_target_pairs={{0,2},{2,4},{4,6},{6,0},{1,3},{3,5},{5,7},{7,1},{8,10},{10,12},{12... | collective-permute-start | bytes 786440 | tf_op jit(solution)/shard_map/ppermute | solution.py:508

commit v4 on v3

--- a/solution.py
+++ b/solution.py
@@ -282,7 +282,7 @@
 
 
 def early_kernel(
-    meta, images, own_screens, got_screens, right_in, left_in,
+    meta, images, own_screens, near_half, far_half, right_in, left_in,
     canvas, screens, edge_u, edge_v, corner,
     labels, raw, right, left, tall, listing, sems,
 ):
@@ -290,7 +290,8 @@
     meta_copies = [pltpu.make_async_copy(meta, labels, sems.at[0])]
     fetches = [
         pltpu.make_async_copy(own_screens, raw.at[:here], sems.at[2]),
-        pltpu.make_async_copy(got_screens, raw.at[here:], sems.at[3]),
+        pltpu.make_async_copy(near_half, raw.at[here : here + here // 2], sems.at[3]),
+        pltpu.make_async_copy(far_half, raw.at[here + here // 2 :], sems.at[1]),
         pltpu.make_async_copy(left_in, left, sems.at[4]),
         pltpu.make_async_copy(right_in, right, sems.at[5]),
     ]
@@ -347,11 +348,15 @@
 ):
     here = screens.shape[0] // 2
     band = lax.axis_index("ch")
+    parity = lax.rem(lax.axis_index("vert"), 2)
 
     def screen_place(station):
         owner = station // here
         local = station - owner * here
-        return jnp.where(owner == band, local, here + local)
+        part = here // 2
+        half_of = local // part
+        moved = here + local - half_of * part + jnp.where(half_of == parity, 0, part)
+        return jnp.where(owner == band, local, moved)
 
     def block(number):
         index = first + number
@@ -435,7 +440,10 @@
     anywhere = pl.BlockSpec(memory_space=pl.ANY)
     n_ch, n_au, n_vert = (lax.axis_size(axis) for axis in ("ch", "au", "vert"))
     here = screens.shape[0]
-    got_screens = lax.ppermute(screens, "ch", [(i, (i + 1) % n_ch) for i in range(n_ch)])
+    parity = lax.rem(lax.axis_index("vert"), 2)
+    chosen = lax.dynamic_slice_in_dim(screens, parity * (here // 2), here // 2, 0)
+    near_half = lax.ppermute(chosen, "ch", [(i, (i + 1) % n_ch) for i in range(n_ch)])
+    far_half = lax.ppermute(near_half, "vert", [(i, i ^ 1) for i in range(n_vert)])
 
     packed, meta = pl.pallas_call(
         pack_kernel,
@@ -496,14 +504,14 @@
             jax.ShapeDtypeStruct((8, TU // 2, 128), BF),
             jax.ShapeDtypeStruct((8, S // 2, 128), BF),
         ),
-        in_specs=[anywhere, vmem] + [anywhere] * 4,
+        in_specs=[anywhere, vmem] + [anywhere] * 5,
         out_specs=(vmem,) * 5,
         scratch_shapes=labels
         + [pltpu.VMEM((2 * here, 4, S * S), BF)]
         + table_scratch
         + [pltpu.VMEM((2, 4 * S, 128), F32), listing, pltpu.SemaphoreType.DMA((6,))],
         compiler_params=pltpu.CompilerParams(vmem_limit_bytes=12 << 20),
-    )(got_meta, images, screens, got_screens, right, left)
+    )(got_meta, images, screens, near_half, far_half, right, left)
     got_u = lax.ppermute(edge_u, "au", [(i, (i + 1) % n_au) for i in range(n_au)])
     got_v = lax.ppermute(edge_v, "vert", [(i, (i + 1) % n_vert) for i in range(n_vert)])
     diagonal = [

time: 52.5 us -> 54.8 us (1.044)
  the two profiles are of different devices: /device:TPU:1 before, /device:TPU:0 now
where the time goes in v4:
time: 54.8 us; the launch traced here: 55.8 us
  Pallas kernels  40.7 us (74%)
  starting transfers between devices  9.23 us (17%)
  local copies, waits for them, and re-layouts  2.89 us (5%)
  waiting for transfers between devices  2.8 us (5%)
    pallas_call x1, Pallas kernels, body(): pl.pallas_call(early_kernel, out_shape=(canvas_shape, jax.ShapeDtypeStruc...  11.2 us
    pallas_call x1, Pallas kernels, body(): pl.pallas_call(image_kernel, out_shape=jax.ShapeDtypeStruct((SLOTS + 2, 4...  9.8 us
    pallas_call x1, Pallas kernels, body(): pl.pallas_call(late_kernel, out_shape=(canvas_shape, jax.ShapeDtypeStruct...  9.39 us
    pallas_call x1, Pallas kernels, body(): pl.pallas_call(exchange_kernel, out_shape=(jax.ShapeDtypeStruct((SLOTS, 8...  6.91 us
    ppermute x1, starting transfers between devices, body(): lax.ppermute(edge_v, 'vert', [(i, (i + 1) % n_vert) for i in range(n_vert)])  3.36 us
    ppermute x1, starting transfers between devices, body(): lax.ppermute(chosen, 'ch', [(i, (i + 1) % n_ch) for i in range(n_ch)])  3.03 us
    ppermute x1, waiting for transfers between devices, body(): lax.ppermute(chosen, 'ch', [(i, (i + 1) % n_ch) for i in range(n_ch)])  2.79 us
    ppermute x1, starting transfers between devices, body(): lax.ppermute(edge_u, 'au', [(i, (i + 1) % n_au) for i in range(n_au)])  2.76 us
  transfers between devices with their start and end apart: 5, of which 1 were waited for; matrix products, arithmetic and copies ran while one was open for 0% of the time, Pallas kernels for 51%

profile of v4, /device:TPU:0, one launch (start us, length us, event | category | flops | bytes accessed | tf_op | source)
XLA Modules:
  0.0 55.8 jit_solution(2538910680052916255)
XLA Ops:
  0.0 1.2 %constant_dynamic-slice_fusion = bf16[16,4,4096]{2,1,0:T(4,128)(2,1)S(1)} fusion(bf16[32,4,4096]{2,1,0:T(4,128)(2,1)} %own_screens.1, s32[]{:T(128)S(6)} %select_n.3), kind=kLoop, calls=%fused_computation | loop fusion | bytes 1048580 | tf_op jit(solution)/shard_map/dynamic_slice | solution.py:444
  1.2 3.0 %collective-permute-start = (bf16[16,4,4096]{2,1,0:T(4,128)(2,1)S(1)}, bf16[16,4,4096]{2,1,0:T(4,128)(2,1)S(1)}, u32[]{:S(2)}, u32[]{:S(2)}) collective-permute-start(bf16[16,4,4096]{2,1,0:T(4,128)(2,1)S(1)} %constant_dynamic-slice_fusion), channel_id=1, source_target_pairs={{0,1},{1,0},{2,3},{3,2},{4,5},{5,4},{6,7},{7,6},{8,9},{9,8},{10,11... | collective-permute-start | bytes 1572872 | tf_op jit(solution)/shard_map/ppermute | solution.py:445
  4.3 2.2 %shard_map.100 = (bf16[40,8,256]{2,1,0:T(8,128)(2,1)}, f32[40,128]{1,0:T(8,128)}) custom-call(s32[32]{0:T(128)} %bitcast.4, s32[32]{0:T(128)} %off_u.1, s32[32]{0:T(128)} %off_v.1, s32[32]{0:T(128)} %base.1, s32[2,2016]{1,0:T(2,128)} %pairs.1, bf16[32,8,256]{2,1,0:T(8,128)(2,1)} %data.1, bf16[2,8,32]{2,1,0:T(8,128)(2,1)} %bitcast.3), custom_call_target="tpu_custom_call" | custom-call | tf_op jit(solution)/shard_map/pallas_call | solution.py:448
  6.5 6.9 %shard_map.101 = (bf16[40,8,256]{2,1,0:T(8,128)(2,1)}, f32[40,128]{1,0:T(8,128)}) custom-call(bf16[40,8,256]{2,1,0:T(8,128)(2,1)} %get-tuple-element.16.data, f32[40,128]{1,0:T(8,128)} %get-tuple-element.17.meta), custom_call_target="tpu_custom_call" | custom-call | tf_op jit(solution)/shard_map/pallas_call | solution.py:461
  13.4 2.8 %collective-permute-done.near_half = bf16[16,4,4096]{2,1,0:T(4,128)(2,1)S(1)} collective-permute-done((bf16[16,4,4096]{2,1,0:T(4,128)(2,1)S(1)}, bf16[16,4,4096]{2,1,0:T(4,128)(2,1)S(1)}, u32[]{:S(2)}, u32[]{:S(2)}) %collective-permute-start) | collective-permute-done | bytes 524320 | tf_op jit(solution)/shard_map/ppermute | solution.py:445
  16.2 0.0 collective-permute-start.1
  16.2 0.0 copy-start.3
  16.2 0.7 %copy-done.3 = f32[40,128]{1,0:T(8,128)S(1)} copy-done((f32[40,128]{1,0:T(8,128)S(1)}, f32[40,128]{1,0:T(8,128)}, u32[]{:S(2)}) %copy-start.3) | copy-done | bytes 20504
  16.9 0.0 copy-start.4
  16.9 0.9 %copy-done.4 = bf16[40,8,256]{2,1,0:T(8,128)(2,1)S(1)} copy-done((bf16[40,8,256]{2,1,0:T(8,128)(2,1)S(1)}, bf16[40,8,256]{2,1,0:T(8,128)(2,1)}, u32[]{:S(2)}) %copy-start.4) | copy-done | bytes 163864
  17.9 9.8 %shard_map.102.images = bf16[42,256,128]{2,1,0:T(8,128)(2,1)S(1)} custom-call(f32[40,128]{1,0:T(8,128)S(1)} %copy-done.3, bf16[40,8,256]{2,1,0:T(8,128)(2,1)S(1)} %copy-done.4), custom_call_target="tpu_custom_call" | custom-call | flops 10737418240 | bytes 8388608 | tf_op jit(solution)/shard_map/pallas_call | solution.py:478
  27.7 0.0 collective-permute-done.1.far_half
  27.7 0.0 copy-done
  27.7 0.0 copy-done.1
  27.7 0.0 copy-done.2
  27.7 11.2 %shard_map.103 = (f32[8,392,384]{2,1,0:T(8,128)S(1)}, bf16[64,2,64,128]{3,2,1,0:T(8,128)(2,1)S(1)}, bf16[8,64,256]{2,1,0:T(8,128)(2,1)S(1)}, bf16[8,128,128]{2,1,0:T(8,128)(2,1)S(1)}, bf16[8,32,128]{2,1,0:T(8,128)(2,1)S(1)}) custom-call(f32[40,128]{1,0:T(8,128)S(1)} %copy-done.3, bf16[42,256,128]{2,1,0:T(8,128)(2,1)S(1)} %shard_map.102.images, ...), custom_call_target="tpu_custom_call" | custom-call | tf_op jit(solution)/shard_map/pallas_call | solution.py:498
  38.9 0.1 collective-permute-start.4
  39.0 2.8 %collective-permute-start.2 = (bf16[8,64,256]{2,1,0:T(8,128)(2,1)S(1)}, bf16[8,64,256]{2,1,0:T(8,128)(2,1)S(1)}, u32[]{:S(2)}, u32[]{:S(2)}) collective-permute-start(bf16[8,64,256]{2,1,0:T(8,128)(2,1)S(1)} %get-tuple-element.24), channel_id=1, source_target_pairs={{0,8},{8,16},{16,24},{24,0},{1,9},{9,17},{17,25},{25,1},{2,10},{10... | collective-permute-start | bytes 786440 | tf_op jit(solution)/shard_map/ppermute | solution.py:515
  41.7 3.4 %collective-permute-start.3 = (bf16[8,128,128]{2,1,0:T(8,128)(2,1)S(1)}, bf16[8,128,128]{2,1,0:T(8,128)(2,1)S(1)}, u32[]{:S(2)}, u32[]{:S(2)}) collective-permute-start(bf16[8,128,128]{2,1,0:T(8,128)(2,1)S(1)} %get-tuple-element.25), channel_id=1, source_target_pairs={{0,2},{2,4},{4,6},{6,0},{1,3},{3,5},{5,7},{7,1},{8,10},{10,12},{12... | collective-permute-start | bytes 786440 | tf_op jit(solution)/shard_map/ppermute | solution.py:516
  45.1 9.4 %shard_map.104 = (f32[8,392,384]{2,1,0:T(8,128)S(1)}, f32[8,256,256]{2,1,0:T(8,128)}) custom-call(f32[40,128]{1,0:T(8,128)S(1)} %copy-done.3, bf16[42,256,128]{2,1,0:T(8,128)(2,1)S(1)} %shard_map.102.images, f32[8,392,384]{2,1,0:T(8,128)S(1)} %get-tuple-element.20.canvas_in, ...), custom_call_target="tpu_custom_call", output_to_operand_aliasing={{0}: (2, {})} | custom-call | flops 10737418240 | bytes 8388608 | tf_op jit(solution)/shard_map/pallas_call | solution.py:523
  54.5 0.0 collective-permute-done.4.got_c
  54.5 0.0 collective-permute-done.2.got_u
  54.5 0.0 collective-permute-done.3.got_v
  54.5 1.3 %shard_map.105 = f32[8,256,256]{2,1,0:T(8,128)} custom-call(f32[8,256,256]{2,1,0:T(8,128)} %get-tuple-element.22.tile, f32[8,392,384]{2,1,0:T(8,128)S(1)} %get-tuple-element.23.canvas, bf16[8,64,256]{2,1,0:T(8,128)(2,1)S(1)} %collective-permute-done.2.got_u, bf16[8,128,128]{2,1,0:T(8,128)(2,1)S(1)} %collective-permute-done.3.got_v, ...), custom_call_target="tpu_custom_call", output_to_operand_aliasing={{}: (0, {})} | custom-call | tf_op jit(solution)/shard_map/pallas_call | solution.py:535
  (3 shorter events, 0.0 us)
Async XLA Ops:
  1.2 15.0 %collective-permute-start = (bf16[16,4,4096]{2,1,0:T(4,128)(2,1)S(1)}, bf16[16,4,4096]{2,1,0:T(4,128)(2,1)S(1)}, u32[]{:S(2)}, u32[]{:S(2)}) collective-permute-start(bf16[16,4,4096]{2,1,0:T(4,128)(2,1)S(1)} %constant_dynamic-slice_fusion), channel_id=1, source_target_pairs={{0,1},{1,0},{2,3},{3,2},{4,5},{5,4},{6,7},{7,6},{8,9},{9,8},{10,11... | collective-permute-start | bytes 1572872 | tf_op jit(solution)/shard_map/ppermute | solution.py:445
  16.2 11.5 %collective-permute-start.1 = (bf16[16,4,4096]{2,1,0:T(4,128)(2,1)S(1)}, bf16[16,4,4096]{2,1,0:T(4,128)(2,1)S(1)}, u32[]{:S(2)}, u32[]{:S(2)}) collective-permute-start(bf16[16,4,4096]{2,1,0:T(4,128)(2,1)S(1)} %collective-permute-done.near_half), channel_id=1, source_target_pairs={{0,2},{2,0},{4,6},{6,4},{1,3},{3,1},{5,7},{7,5},{8,10},{10,8},{12,... | collective-permute-start | bytes 1572872 | tf_op jit(solution)/shard_map/ppermute | solution.py:446
  16.2 0.7 %copy-start.3 = (f32[40,128]{1,0:T(8,128)S(1)}, f32[40,128]{1,0:T(8,128)}, u32[]{:S(2)}) copy-start(f32[40,128]{1,0:T(8,128)} %get-tuple-element.18.meta) | copy-start | bytes 61444
  16.9 0.9 %copy-start.4 = (bf16[40,8,256]{2,1,0:T(8,128)(2,1)S(1)}, bf16[40,8,256]{2,1,0:T(8,128)(2,1)}, u32[]{:S(2)}) copy-start(bf16[40,8,256]{2,1,0:T(8,128)(2,1)} %get-tuple-element.19.data) | copy-start | bytes 491524
  17.8 9.8 %copy-start = (bf16[32,4,4096]{2,1,0:T(4,128)(2,1)S(1)}, bf16[32,4,4096]{2,1,0:T(4,128)(2,1)}, u32[]{:S(2)}) copy-start(bf16[32,4,4096]{2,1,0:T(4,128)(2,1)} %own_screens.1) | copy-start | bytes 3145732
  17.8 9.8 %copy-start.1 = (bf16[8,144,128]{2,1,0:T(8,128)(2,1)S(1)}, bf16[8,144,128]{2,1,0:T(8,128)(2,1)}, u32[]{:S(2)}) copy-start(bf16[8,144,128]{2,1,0:T(8,128)(2,1)} %constant.21.clone.left_in) | copy-start | bytes 884740
  17.9 9.8 %copy-start.2 = (f32[128,256]{1,0:T(8,128)S(1)}, f32[128,256]{1,0:T(8,128)}, u32[]{:S(2)}) copy-start(f32[128,256]{1,0:T(8,128)} %constant.20.clone.right_in) | copy-start | bytes 393220
  38.9 15.6 %collective-permute-start.4 = (bf16[8,32,128]{2,1,0:T(8,128)(2,1)S(1)}, bf16[8,32,128]{2,1,0:T(8,128)(2,1)S(1)}, u32[]{:S(2)}, u32[]{:S(2)}) collective-permute-start(bf16[8,32,128]{2,1,0:T(8,128)(2,1)S(1)} %get-tuple-element.26), channel_id=1, source_target_pairs={{0,10},{2,12},{4,14},{6,8},{8,18},{10,20},{12,22},{14,16},{16,26},... | collective-permute-start | bytes 196616 | tf_op jit(solution)/shard_map/ppermute | solution.py:522
  39.0 15.5 %collective-permute-start.2 = (bf16[8,64,256]{2,1,0:T(8,128)(2,1)S(1)}, bf16[8,64,256]{2,1,0:T(8,128)(2,1)S(1)}, u32[]{:S(2)}, u32[]{:S(2)}) collective-permute-start(bf16[8,64,256]{2,1,0:T(8,128)(2,1)S(1)} %get-tuple-element.24), channel_id=1, source_target_pairs={{0,8},{8,16},{16,24},{24,0},{1,9},{9,17},{17,25},{25,1},{2,10},{10... | collective-permute-start | bytes 786440 | tf_op jit(solution)/shard_map/ppermute | solution.py:515
  41.7 12.8 %collective-permute-start.3 = (bf16[8,128,128]{2,1,0:T(8,128)(2,1)S(1)}, bf16[8,128,128]{2,1,0:T(8,128)(2,1)S(1)}, u32[]{:S(2)}, u32[]{:S(2)}) collective-permute-start(bf16[8,128,128]{2,1,0:T(8,128)(2,1)S(1)} %get-tuple-element.25), channel_id=1, source_target_pairs={{0,2},{2,4},{4,6},{6,0},{1,3},{3,5},{5,7},{7,1},{8,10},{10,12},{12... | collective-permute-start | bytes 786440 | tf_op jit(solution)/shard_map/ppermute | solution.py:516

commit v5 on v3

--- a/solution.py
+++ b/solution.py
@@ -197,7 +197,9 @@
     return feeds
 
 
-def image_kernel(meta, data, images, labels, spread, mult, listing, sems):
+def image_kernel(
+    meta, data, own_screens, images, arranged, labels, spread, tall, mult, listing, sems
+):
     copy = pltpu.make_async_copy(meta, labels, sems.at[0])
     copy.start()
     band = lax.axis_index("ch")
@@ -274,6 +276,15 @@
 
     lax.fori_loop(0, early + late, loop, 0)
 
+    def arrange(pair, carry):
+        for i in range(2):
+            feeds = arrange_station(own_screens[2 * pair + i], tall.at[i])
+            for f in range(2):
+                arranged[2 * pair + i, f] = feeds[f]
+        return carry
+
+    lax.fori_loop(0, own_screens.shape[0] // 2, arrange, 0)
+
 
 def folded(x):
     middle = x.shape[1] // 2
@@ -282,15 +293,15 @@
 
 
 def early_kernel(
-    meta, images, own_screens, got_screens, right_in, left_in,
+    meta, images, arranged, got_screens, right_in, left_in,
     canvas, screens, edge_u, edge_v, corner,
     labels, raw, right, left, tall, listing, sems,
 ):
-    here = own_screens.shape[0]
+    here = arranged.shape[0]
     meta_copies = [pltpu.make_async_copy(meta, labels, sems.at[0])]
     fetches = [
-        pltpu.make_async_copy(own_screens, raw.at[:here], sems.at[2]),
-        pltpu.make_async_copy(got_screens, raw.at[here:], sems.at[3]),
+        pltpu.make_async_copy(arranged, screens.at[:here], sems.at[2]),
+        pltpu.make_async_copy(got_screens, raw, sems.at[3]),
         pltpu.make_async_copy(left_in, left, sems.at[4]),
         pltpu.make_async_copy(right_in, right, sems.at[5]),
     ]
@@ -307,10 +318,10 @@
         for i in range(2):
             feeds = arrange_station(raw[2 * pair + i], tall.at[i])
             for f in range(2):
-                screens[2 * pair + i, f] = feeds[f]
+                screens[here + 2 * pair + i, f] = feeds[f]
         return carry
 
-    lax.fori_loop(0, here, arrange, 0)
+    lax.fori_loop(0, here // 2, arrange, 0)
     grid_blocks(images, screens, canvas, right, left, listing, early, 0, 0)
     edge_u[...] = canvas[:, TU : TU + S, :TV].astype(BF)
     edge_v[...] = folded(canvas[:, :TU, TV:])
@@ -467,14 +478,18 @@
     )(packed, meta)
     labels = [pltpu.SMEM((SLOTS, 128), F32)]
     listing = pltpu.SMEM((8, 2 * LATER), jnp.int32)
-    images = pl.pallas_call(
+    images, arranged = pl.pallas_call(
         image_kernel,
-        out_shape=jax.ShapeDtypeStruct((SLOTS + 2, 4 * S, 2 * S), BF),
-        in_specs=[vmem, vmem],
-        out_specs=vmem,
+        out_shape=(
+            jax.ShapeDtypeStruct((SLOTS + 2, 4 * S, 2 * S), BF),
+            jax.ShapeDtypeStruct((here, 2, S, 2 * S), BF),
+        ),
+        in_specs=[vmem] * 3,
+        out_specs=(vmem, vmem),
         scratch_shapes=labels
         + [
             pltpu.VMEM((SLOTS, 2 * K), F32),
+            pltpu.VMEM((2, 4 * S, 128), F32),
             pltpu.VMEM((32, K), F32),
             listing,
             pltpu.SemaphoreType.DMA((1,)),
@@ -483,7 +498,7 @@
         cost_estimate=pl.CostEstimate(
             flops=SLOTS * 2 * 256 * 512 * 128 * 8, bytes_accessed=8 << 20, transcendentals=0
         ),
-    )(got_meta, got_data)
+    )(got_meta, got_data, screens)
     right, left = jnp.asarray(right_table()), jnp.asarray(left_table())
     table_scratch = [pltpu.VMEM((2 * S, 256), F32), pltpu.VMEM((8, 2 * ROWS, 2 * S), BF)]
     canvas_shape = jax.ShapeDtypeStruct((8, TU + S + ROWS, TV + 128), F32)
@@ -499,11 +514,11 @@
         in_specs=[anywhere, vmem] + [anywhere] * 4,
         out_specs=(vmem,) * 5,
         scratch_shapes=labels
-        + [pltpu.VMEM((2 * here, 4, S * S), BF)]
+        + [pltpu.VMEM((here, 4, S * S), BF)]
         + table_scratch
         + [pltpu.VMEM((2, 4 * S, 128), F32), listing, pltpu.SemaphoreType.DMA((6,))],
         compiler_params=pltpu.CompilerParams(vmem_limit_bytes=12 << 20),
-    )(got_meta, images, screens, got_screens, right, left)
+    )(got_meta, images, arranged, got_screens, right, left)
     got_u = lax.ppermute(edge_u, "au", [(i, (i + 1) % n_au) for i in range(n_au)])
     got_v = lax.ppermute(edge_v, "vert", [(i, (i + 1) % n_vert) for i in range(n_vert)])
     diagonal = [

time: 52.5 us -> 52.4 us (level); the launches traced: 52.8 us -> 51.9 us
  waiting for transfers between devices: 1.45 us -> 0.01 us
  local copies, waits for them, and re-layouts: 1.65 us -> 2.87 us
  Pallas kernels: 42 us -> 40.9 us
    pallas_call x1, Pallas kernels: 9.8 us -> 7.4 us  [body(): pl.pallas_call(early_kernel, out_shape=(canvas_shape, jax.ShapeDtypeStruc...]
    ppermute x1, waiting for transfers between devices: 1.45 us -> 0.01 us  [body(): lax.ppermute(screens, 'ch', [(i, (i + 1) % n_ch) for i in range(n_ch)])]
    pallas_call x1, Pallas kernels: 9.79 us -> 11.1 us  [body(): pl.pallas_call(image_kernel, out_shape=(jax.ShapeDtypeStruct((SLOTS + 2,...]
    unnamed x12, local copies, waits for them, and re-layouts: 1.65 us -> 2.87 us
    ppermute x1, starting transfers between devices: 0.57 us -> 1.31 us  [body(): lax.ppermute(edge_u, 'au', [(i, (i + 1) % n_au) for i in range(n_au)])]
  transfers between devices with their start and end apart: 4 -> 4, of which waited for: 1 -> 0; matrix products, arithmetic and copies ran while one was open for 0% -> 0% of each run, Pallas kernels for 59% -> 62%
where the time goes in v5:
time: 52.4 us; the launch traced here: 51.9 us
  Pallas kernels  40.9 us (78%)
  starting transfers between devices  8.06 us (15%)
  local copies, waits for them, and re-layouts  2.87 us (5%)
    pallas_call x1, Pallas kernels, body(): pl.pallas_call(image_kernel, out_shape=(jax.ShapeDtypeStruct((SLOTS + 2,...  11.1 us
    pallas_call x1, Pallas kernels, body(): pl.pallas_call(late_kernel, out_shape=(canvas_shape, jax.ShapeDtypeStruct...  11 us
    pallas_call x1, Pallas kernels, body(): pl.pallas_call(exchange_kernel, out_shape=(jax.ShapeDtypeStruct((SLOTS, 8...  7.96 us
    pallas_call x1, Pallas kernels, body(): pl.pallas_call(early_kernel, out_shape=(canvas_shape, jax.ShapeDtypeStruc...  7.4 us
    ppermute x1, starting transfers between devices, body(): got_c = lax.ppermute(corner, ('au', 'vert'), diagonal)  4.56 us
    unnamed x12, local copies, waits for them, and re-layouts  2.87 us
    pallas_call x1, Pallas kernels, body(): pl.pallas_call(pack_kernel, out_shape=(jax.ShapeDtypeStruct((SLOTS, 8, K)...  2.22 us
    ppermute x1, starting transfers between devices, body(): lax.ppermute(screens, 'ch', [(i, (i + 1) % n_ch) for i in range(n_ch)])  2.07 us
  transfers between devices with their start and end apart: 4, of which 0 were waited for; matrix products, arithmetic and copies ran while one was open for 0% of the time, Pallas kernels for 62%

profile of v5, /device:TPU:1, one launch (start us, length us, event | category | flops | bytes accessed | tf_op | source)
XLA Modules:
  0.0 51.9 jit_solution(12807897762601224464)
XLA Ops:
  0.0 2.1 %collective-permute-start = (bf16[32,4,4096]{2,1,0:T(4,128)(2,1)}, bf16[32,4,4096]{2,1,0:T(4,128)(2,1)S(1)}, u32[]{:S(2)}, u32[]{:S(2)}) collective-permute-start(bf16[32,4,4096]{2,1,0:T(4,128)(2,1)} %own_screens.1), channel_id=1, source_target_pairs={{0,1},{1,0},{2,3},{3,2},{4,5},{5,4},{6,7},{7,6},{8,9},{9,8},{10,11... | collective-permute-start | bytes 3145736 | tf_op jit(solution)/shard_map/ppermute | solution.py:449
  2.1 2.2 %shard_map.100 = (bf16[40,8,256]{2,1,0:T(8,128)(2,1)}, f32[40,128]{1,0:T(8,128)}) custom-call(s32[32]{0:T(128)} %bitcast.4, s32[32]{0:T(128)} %off_u.1, s32[32]{0:T(128)} %off_v.1, s32[32]{0:T(128)} %base.1, s32[2,2016]{1,0:T(2,128)} %pairs.1, bf16[32,8,256]{2,1,0:T(8,128)(2,1)} %data.1, bf16[2,8,32]{2,1,0:T(8,128)(2,1)} %bitcast.3), custom_call_target="tpu_custom_call" | custom-call | tf_op jit(solution)/shard_map/pallas_call | solution.py:451
  4.3 8.0 %shard_map.101 = (bf16[40,8,256]{2,1,0:T(8,128)(2,1)}, f32[40,128]{1,0:T(8,128)}) custom-call(bf16[40,8,256]{2,1,0:T(8,128)(2,1)} %get-tuple-element.18.data, f32[40,128]{1,0:T(8,128)} %get-tuple-element.19.meta), custom_call_target="tpu_custom_call" | custom-call | tf_op jit(solution)/shard_map/pallas_call | solution.py:464
  12.3 0.0 copy-start.2
  12.3 0.7 %copy-done.2 = f32[40,128]{1,0:T(8,128)S(1)} copy-done((f32[40,128]{1,0:T(8,128)S(1)}, f32[40,128]{1,0:T(8,128)}, u32[]{:S(2)}) %copy-start.2) | copy-done | bytes 20504
  13.0 0.0 copy-start.4
  13.0 1.2 %copy-done.4 = bf16[32,4,4096]{2,1,0:T(4,128)(2,1)S(1)} copy-done((bf16[32,4,4096]{2,1,0:T(4,128)(2,1)S(1)}, bf16[32,4,4096]{2,1,0:T(4,128)(2,1)}, u32[]{:S(2)}) %copy-start.4) | copy-done | bytes 1048600
  14.2 0.0 copy-start.5
  14.2 0.9 %copy-done.5 = bf16[40,8,256]{2,1,0:T(8,128)(2,1)S(1)} copy-done((bf16[40,8,256]{2,1,0:T(8,128)(2,1)S(1)}, bf16[40,8,256]{2,1,0:T(8,128)(2,1)}, u32[]{:S(2)}) %copy-start.5) | copy-done | bytes 163864
  15.1 11.1 %shard_map.102 = (bf16[42,256,128]{2,1,0:T(8,128)(2,1)S(1)}, bf16[32,2,64,128]{3,2,1,0:T(8,128)(2,1)S(1)}) custom-call(f32[40,128]{1,0:T(8,128)S(1)} %copy-done.2, bf16[40,8,256]{2,1,0:T(8,128)(2,1)S(1)} %copy-done.5, bf16[32,4,4096]{2,1,0:T(4,128)(2,1)S(1)} %copy-done.4), custom_call_target="tpu_custom_call" | custom-call | flops 10737418240 | bytes 8388608 | tf_op jit(solution)/shard_map/pallas_call | solution.py:481
  26.2 0.0 copy-start.3
  26.2 0.0 collective-permute-done.got_screens
  26.2 0.0 copy-done
  26.2 0.0 copy-done.1
  26.3 7.4 %shard_map.103 = (f32[8,392,384]{2,1,0:T(8,128)S(1)}, bf16[64,2,64,128]{3,2,1,0:T(8,128)(2,1)S(1)}, bf16[8,64,256]{2,1,0:T(8,128)(2,1)S(1)}, bf16[8,128,128]{2,1,0:T(8,128)(2,1)S(1)}, bf16[8,32,128]{2,1,0:T(8,128)(2,1)S(1)}) custom-call(f32[40,128]{1,0:T(8,128)S(1)} %copy-done.2, bf16[42,256,128]{2,1,0:T(8,128)(2,1)S(1)} %get-tuple-element.22.images, ...), custom_call_target="tpu_custom_call" | custom-call | tf_op jit(solution)/shard_map/pallas_call | solution.py:505
  33.7 4.6 %collective-permute-start.3 = (bf16[8,32,128]{2,1,0:T(8,128)(2,1)S(1)}, bf16[8,32,128]{2,1,0:T(8,128)(2,1)S(1)}, u32[]{:S(2)}, u32[]{:S(2)}) collective-permute-start(bf16[8,32,128]{2,1,0:T(8,128)(2,1)S(1)} %get-tuple-element.30), channel_id=1, source_target_pairs={{0,10},{2,12},{4,14},{6,8},{8,18},{10,20},{12,22},{14,16},{16,26},... | collective-permute-start | bytes 196616 | tf_op jit(solution)/shard_map/ppermute | solution.py:529
  38.2 1.3 %collective-permute-start.1 = (bf16[8,64,256]{2,1,0:T(8,128)(2,1)S(1)}, bf16[8,64,256]{2,1,0:T(8,128)(2,1)S(1)}, u32[]{:S(2)}, u32[]{:S(2)}) collective-permute-start(bf16[8,64,256]{2,1,0:T(8,128)(2,1)S(1)} %get-tuple-element.28), channel_id=1, source_target_pairs={{0,8},{8,16},{16,24},{24,0},{1,9},{9,17},{17,25},{25,1},{2,10},{10... | collective-permute-start | bytes 786440 | tf_op jit(solution)/shard_map/ppermute | solution.py:522
  39.5 0.1 collective-permute-start.2
  39.7 0.0 copy-done.3
  39.7 11.0 %shard_map.104 = (f32[8,392,384]{2,1,0:T(8,128)S(1)}, f32[8,256,256]{2,1,0:T(8,128)}) custom-call(f32[40,128]{1,0:T(8,128)S(1)} %copy-done.3, bf16[42,256,128]{2,1,0:T(8,128)(2,1)S(1)} %get-tuple-element.22.images, f32[8,392,384]{2,1,0:T(8,128)S(1)} %get-tuple-element.24.canvas_in, ...), custom_call_target="tpu_custom_call", output_to_operand_aliasing={{0}: (2, {})} | custom-call | flops 10737418240 | bytes 8388608 | tf_op jit(solution)/shard_map/pallas_call | solution.py:530
  50.6 0.0 collective-permute-done.3.got_c
  50.6 0.0 collective-permute-done.1.got_u
  50.7 0.0 collective-permute-done.2.got_v
  50.7 1.3 %shard_map.105 = f32[8,256,256]{2,1,0:T(8,128)} custom-call(f32[8,256,256]{2,1,0:T(8,128)} %get-tuple-element.26.tile, f32[8,392,384]{2,1,0:T(8,128)S(1)} %get-tuple-element.27.canvas, bf16[8,64,256]{2,1,0:T(8,128)(2,1)S(1)} %collective-permute-done.1.got_u, bf16[8,128,128]{2,1,0:T(8,128)(2,1)S(1)} %collective-permute-done.2.got_v, ...), custom_call_target="tpu_custom_call", output_to_operand_aliasing={{}: (0, {})} | custom-call | tf_op jit(solution)/shard_map/pallas_call | solution.py:542
  (2 shorter events, 0.0 us)
Async XLA Ops:
  0.0 26.2 %collective-permute-start = (bf16[32,4,4096]{2,1,0:T(4,128)(2,1)}, bf16[32,4,4096]{2,1,0:T(4,128)(2,1)S(1)}, u32[]{:S(2)}, u32[]{:S(2)}) collective-permute-start(bf16[32,4,4096]{2,1,0:T(4,128)(2,1)} %own_screens.1), channel_id=1, source_target_pairs={{0,1},{1,0},{2,3},{3,2},{4,5},{5,4},{6,7},{7,6},{8,9},{9,8},{10,11... | collective-permute-start | bytes 3145736 | tf_op jit(solution)/shard_map/ppermute | solution.py:449
  12.3 0.7 %copy-start.2 = (f32[40,128]{1,0:T(8,128)S(1)}, f32[40,128]{1,0:T(8,128)}, u32[]{:S(2)}) copy-start(f32[40,128]{1,0:T(8,128)} %get-tuple-element.20.meta) | copy-start | bytes 61444
  13.0 1.2 %copy-start.4 = (bf16[32,4,4096]{2,1,0:T(4,128)(2,1)S(1)}, bf16[32,4,4096]{2,1,0:T(4,128)(2,1)}, u32[]{:S(2)}) copy-start(bf16[32,4,4096]{2,1,0:T(4,128)(2,1)} %own_screens.1) | copy-start | bytes 3145732
  14.2 0.9 %copy-start.5 = (bf16[40,8,256]{2,1,0:T(8,128)(2,1)S(1)}, bf16[40,8,256]{2,1,0:T(8,128)(2,1)}, u32[]{:S(2)}) copy-start(bf16[40,8,256]{2,1,0:T(8,128)(2,1)} %get-tuple-element.21.data) | copy-start | bytes 491524
  15.1 11.1 %copy-start = (bf16[8,144,128]{2,1,0:T(8,128)(2,1)S(1)}, bf16[8,144,128]{2,1,0:T(8,128)(2,1)}, u32[]{:S(2)}) copy-start(bf16[8,144,128]{2,1,0:T(8,128)(2,1)} %constant.5.clone.left_in) | copy-start | bytes 884740
  15.1 11.1 %copy-start.1 = (f32[128,256]{1,0:T(8,128)S(1)}, f32[128,256]{1,0:T(8,128)}, u32[]{:S(2)}) copy-start(f32[128,256]{1,0:T(8,128)} %constant.4.clone.right_in) | copy-start | bytes 393220
  26.2 13.4 %copy-start.3 = (f32[40,128]{1,0:T(8,128)S(1)}, f32[40,128]{1,0:T(8,128)}, u32[]{:S(2)}) copy-start(f32[40,128]{1,0:T(8,128)} %get-tuple-element.20.meta) | copy-start | bytes 61444
  33.7 17.0 %collective-permute-start.3 = (bf16[8,32,128]{2,1,0:T(8,128)(2,1)S(1)}, bf16[8,32,128]{2,1,0:T(8,128)(2,1)S(1)}, u32[]{:S(2)}, u32[]{:S(2)}) collective-permute-start(bf16[8,32,128]{2,1,0:T(8,128)(2,1)S(1)} %get-tuple-element.30), channel_id=1, source_target_pairs={{0,10},{2,12},{4,14},{6,8},{8,18},{10,20},{12,22},{14,16},{16,26},... | collective-permute-start | bytes 196616 | tf_op jit(solution)/shard_map/ppermute | solution.py:529
  38.2 12.4 %collective-permute-start.1 = (bf16[8,64,256]{2,1,0:T(8,128)(2,1)S(1)}, bf16[8,64,256]{2,1,0:T(8,128)(2,1)S(1)}, u32[]{:S(2)}, u32[]{:S(2)}) collective-permute-start(bf16[8,64,256]{2,1,0:T(8,128)(2,1)S(1)} %get-tuple-element.28), channel_id=1, source_target_pairs={{0,8},{8,16},{16,24},{24,0},{1,9},{9,17},{17,25},{25,1},{2,10},{10... | collective-permute-start | bytes 786440 | tf_op jit(solution)/shard_map/ppermute | solution.py:522
  39.5 11.1 %collective-permute-start.2 = (bf16[8,128,128]{2,1,0:T(8,128)(2,1)S(1)}, bf16[8,128,128]{2,1,0:T(8,128)(2,1)S(1)}, u32[]{:S(2)}, u32[]{:S(2)}) collective-permute-start(bf16[8,128,128]{2,1,0:T(8,128)(2,1)S(1)} %get-tuple-element.29), channel_id=1, source_target_pairs={{0,2},{2,4},{4,6},{6,0},{1,3},{3,5},{5,7},{7,1},{8,10},{10,12},{12... | collective-permute-start | bytes 786440 | tf_op jit(solution)/shard_map/ppermute | solution.py:523
